TPU v7x, 32 devices: a whole 2x2x4 slice. The times are simulated.
32 devices in a mesh: dp: 4 (over z), graph: 8 (over y, x, core).
Axes of the slice: x: 2, y: 2, z: 4, core: 2. Of those that a mesh axis runs over, the one named last changes fastest.
Arguments:
- features: float32 [4, 128, 3200], P('dp', 'graph'), may hold values from -6 to 6
- cotangent: float32 [4, 128, 1600], P('dp', 'graph'), may hold values from -6 to 6
- rotation: bfloat16 [4, 114, 1536], P('dp', None, 'graph'), may hold values from -2.6875 to 2.6875
- send_left: int32 [4, 64], P('dp', 'graph'), may hold values from 0 to 16, as said below
- send_right: int32 [4, 64], P('dp', 'graph'), may hold values from 0 to 16, as said below
- edge_src: int32 [4, 1536], P('dp', 'graph'), may hold values from 0 to 31, as said below
- edge_tgt: int32 [4, 1536], P('dp', 'graph'), may hold values from 0 to 15, as said below
- w_zero: bfloat16 [640, 832], P('graph'), may hold values from -0.25 to 0.25
- w_one_re: bfloat16 [512, 256], P('graph'), may hold values from -0.1875 to 0.1875
- w_one_im: bfloat16 [512, 256], P('graph'), may hold values from -0.1875 to 0.1875
- w_two_re: bfloat16 [384, 192], P('graph'), may hold values from -0.21875 to 0.21875
- w_two_im: bfloat16 [384, 192], P('graph'), may hold values from -0.21875 to 0.21875
- w_target: bfloat16 [128, 512], P('graph'), may hold values from -0.5 to 0.5
- alpha_vec: bfloat16 [64, 8], P('graph'), may hold values from -0.75 to 0.75
Outputs:
- attended: bfloat16 [4, 128, 1600], P('dp', 'graph')
- grad_features: float32 [4, 128, 3200], P('dp', 'graph')
- grad_zero: float32 [640, 832], P('graph')
- grad_one_re: float32 [512, 256], P('graph')
- grad_one_im: float32 [512, 256], P('graph')
- grad_two_re: float32 [384, 192], P('graph')
- grad_two_im: float32 [384, 192], P('graph')
- grad_target: float32 [128, 512], P('graph')
- grad_alpha: float32 [64, 8], P('graph')
Inputs may be any that keep to these rules, and one draw needn't show every extreme that they name: `send_left`: filled slots come first and name distinct atoms; the value 16 marks an empty slot; each list holds 4 or more atoms, and in every cell some slab fills all 8 slots. `send_right`: like send_left. `edge_src`: values below 16 are the slab's own atoms; 16 + k is slot k of slab g-1's send_right, 24 + k slot k of slab g+1's send_left; never an empty slot. `edge_tgt`: every atom of a slab is the target of one edge or more.
All inputs are finite; a program needn't handle non-finite values.
Results may differ from a plain program's by a relative error of at most 0.0085.
Values may be sent and summed in bfloat16 or wider, within the bound.
A program may use at most 128 MiB of HBM per device.

v0:
```python
from functools import partial

import jax
import jax.numpy as jnp
from jax import lax
from jax.sharding import PartitionSpec as P


def padded_2(block, sides, width):
    for axis, dim in sides:
        count = lax.axis_size(axis)
        forward = [(i, i + 1) for i in range(count - 1)]
        forward.append((count - 1, 0))
        backward = [(target, source) for source, target in forward]
        low = lax.ppermute(
            lax.slice_in_dim(block, block.shape[dim] - width, None, axis=dim), axis, forward
        )
        high = lax.ppermute(lax.slice_in_dim(block, 0, width, axis=dim), axis, backward)
        block = jnp.concatenate([low, block, high], axis=dim)
    return block


def turn_blocks(rotation, edge_count):
    blocks = []
    offset = 0
    for degree in range(1, 5):
        kept_order = min(degree, 2)
        row_count = 2 * kept_order + 1
        column_count = 2 * degree + 1
        piece_block = rotation[offset : offset + row_count * column_count].astype(jnp.float32)
        blocks.append(piece_block.reshape(row_count, column_count, edge_count))
        offset = offset + row_count * column_count
    return blocks


def apply_block(block, source_part):
    rows_out = []
    for row in range(block.shape[0]):
        total = block[row, 0][:, None] * source_part[:, 0, :]
        for column in range(1, block.shape[1]):
            total = total + block[row, column][:, None] * source_part[:, column, :]
        rows_out.append(total)
    return jnp.stack(rows_out, axis=1)


def apply_back(block, stacked):
    columns_out = []
    for column in range(block.shape[1]):
        total = block[0, column][:, None] * stacked[:, 0, :]
        for row in range(1, block.shape[0]):
            total = total + block[row, column][:, None] * stacked[:, row, :]
        columns_out.append(total)
    return jnp.stack(columns_out, axis=1)


def pick_order(turned, azimuth, degrees, edge_count):
    chosen = jnp.stack(
        [turned[degree][:, min(degree, 2) + azimuth, :] for degree in degrees], axis=1
    )
    return chosen.reshape(edge_count, -1).astype(jnp.bfloat16)


def attend(
    extended,
    w_zero,
    w_one_re,
    w_one_im,
    w_two_re,
    w_two_im,
    w_target,
    alpha_vec,
    rotation,
    edge_src,
    edge_tgt,
    atom_count,
):
    edge_count = edge_src.shape[0]
    channels = w_target.shape[0]
    hidden = w_one_re.shape[1] // 4
    head_count = alpha_vec.shape[1]
    alpha_width = alpha_vec.shape[0]
    blocks = turn_blocks(rotation, edge_count)
    coeffs = extended.reshape(extended.shape[0], 25, channels)
    turned = [jnp.take(coeffs[:, 0:1, :], edge_src, axis=0)]
    for degree in range(1, 5):
        source_part = jnp.take(
            coeffs[:, degree * degree : (degree + 1) * (degree + 1), :], edge_src, axis=0
        )
        turned.append(apply_block(blocks[degree - 1], source_part))
    zero_in = pick_order(turned, 0, range(5), edge_count)
    one_pos = pick_order(turned, 1, range(1, 5), edge_count)
    one_neg = pick_order(turned, -1, range(1, 5), edge_count)
    two_pos = pick_order(turned, 2, range(2, 5), edge_count)
    two_neg = pick_order(turned, -2, range(2, 5), edge_count)
    mixed = jnp.dot(zero_in, w_zero, preferred_element_type=jnp.float32)
    hidden_zero = mixed[:, : 5 * hidden].reshape(edge_count, 5, hidden)
    target_in = extended[:atom_count, :channels].astype(jnp.bfloat16)
    per_atom = jnp.dot(target_in, w_target, preferred_element_type=jnp.float32)
    alpha_pre = mixed[:, 5 * hidden :] + jnp.take(per_atom, edge_tgt, axis=0)
    one_up = jnp.dot(one_pos, w_one_re, preferred_element_type=jnp.float32) - jnp.dot(
        one_neg, w_one_im, preferred_element_type=jnp.float32
    )
    one_down = jnp.dot(one_neg, w_one_re, preferred_element_type=jnp.float32) + jnp.dot(
        one_pos, w_one_im, preferred_element_type=jnp.float32
    )
    two_up = jnp.dot(two_pos, w_two_re, preferred_element_type=jnp.float32) - jnp.dot(
        two_neg, w_two_im, preferred_element_type=jnp.float32
    )
    two_down = jnp.dot(two_neg, w_two_re, preferred_element_type=jnp.float32) + jnp.dot(
        two_pos, w_two_im, preferred_element_type=jnp.float32
    )
    scalar = hidden_zero[:, 0, :]
    gating = jax.nn.sigmoid(scalar)[:, None, :]
    value_zero = jnp.concatenate(
        [jax.nn.silu(scalar)[:, None, :], hidden_zero[:, 1:, :] * gating], axis=1
    )
    one_up = one_up.reshape(edge_count, 4, hidden) * gating
    one_down = one_down.reshape(edge_count, 4, hidden) * gating
    two_up = two_up.reshape(edge_count, 3, hidden) * gating
    two_down = two_down.reshape(edge_count, 3, hidden) * gating
    scores = alpha_pre.reshape(edge_count, head_count, alpha_width)
    centre = scores - jnp.mean(scores, axis=-1, keepdims=True)
    normed = centre * lax.rsqrt(jnp.mean(centre * centre, axis=-1, keepdims=True) + 1e-05)
    activated = normed * (0.2 + 0.8 * jax.nn.sigmoid(normed))
    logits = jnp.einsum(
        "ehc,ch->eh", activated, alpha_vec.astype(jnp.float32), precision=lax.Precision.HIGHEST
    )
    raised = jnp.exp(logits)
    member = (edge_tgt[:, None] == jnp.arange(atom_count, dtype=jnp.int32)[None, :]).astype(
        jnp.float32
    )
    totals = jnp.dot(member.T, raised, precision=lax.Precision.HIGHEST)
    weights = raised / jnp.take(totals, edge_tgt, axis=0)
    spread = jnp.repeat(weights, hidden // head_count, axis=1)[:, None, :]
    value_zero = value_zero * spread
    one_up = one_up * spread
    one_down = one_down * spread
    two_up = two_up * spread
    two_down = two_down * spread
    pieces = [value_zero[:, 0:1, :]]
    for degree in range(1, 5):
        kept_order = min(degree, 2)
        row_list = []
        for azimuth in range(-kept_order, kept_order + 1):
            if azimuth == 0:
                row_list.append(value_zero[:, degree])
            elif azimuth == 1:
                row_list.append(one_up[:, degree - 1])
            elif azimuth == -1:
                row_list.append(one_down[:, degree - 1])
            elif azimuth == 2:
                row_list.append(two_up[:, degree - 2])
            else:
                row_list.append(two_down[:, degree - 2])
        stacked = jnp.stack(row_list, axis=1)
        pieces.append(apply_back(blocks[degree - 1], stacked))
    message = jnp.concatenate(pieces, axis=1).reshape(edge_count, -1).astype(jnp.bfloat16)
    return jnp.dot(member.T.astype(jnp.bfloat16), message, preferred_element_type=jnp.float32)


def body(
    features,
    cotangent,
    rotation,
    send_left,
    send_right,
    edge_src,
    edge_tgt,
    w_zero,
    w_one_re,
    w_one_im,
    w_two_re,
    w_two_im,
    w_target,
    alpha_vec,
):
    full_weights = (
        lax.all_gather(w_zero, "graph", axis=0, tiled=True),
        lax.all_gather(w_one_re, "graph", axis=0, tiled=True),
        lax.all_gather(w_one_im, "graph", axis=0, tiled=True),
        lax.all_gather(w_two_re, "graph", axis=0, tiled=True),
        lax.all_gather(w_two_im, "graph", axis=0, tiled=True),
        lax.all_gather(w_target, "graph", axis=0, tiled=True),
        lax.all_gather(alpha_vec, "graph", axis=0, tiled=True),
    )
    own_rows = features[0]
    atom_count = own_rows.shape[0]
    ghost_count = send_left.shape[1]
    row_width = own_rows.shape[1]
    padded = jnp.concatenate([own_rows, jnp.zeros((1, row_width), jnp.float32)], axis=0)
    outgoing = jnp.concatenate(
        [jnp.take(padded, send_left[0], axis=0), jnp.take(padded, send_right[0], axis=0)], axis=0
    )
    widened = padded_2(outgoing, (("graph", 0),), ghost_count)
    extended = jnp.concatenate(
        [own_rows, widened[:ghost_count], widened[3 * ghost_count :]], axis=0
    )
    local_fn = partial(
        attend,
        rotation=rotation[0],
        edge_src=edge_src[0],
        edge_tgt=edge_tgt[0],
        atom_count=atom_count,
    )
    summed, pullback = jax.vjp(
        local_fn,
        extended,
        full_weights[0],
        full_weights[1],
        full_weights[2],
        full_weights[3],
        full_weights[4],
        full_weights[5],
        full_weights[6],
    )
    pulled = pullback(cotangent[0])
    ext_grad = pulled[0]
    returned = padded_2(
        ext_grad[atom_count:].astype(jnp.bfloat16), (("graph", 0),), ghost_count
    ).astype(jnp.float32)
    collected = jnp.concatenate(
        [ext_grad[:atom_count], jnp.zeros((1, row_width), jnp.float32)], axis=0
    )
    collected = collected.at[send_left[0]].add(returned[:ghost_count])
    collected = collected.at[send_right[0]].add(returned[3 * ghost_count :])
    grad_features = collected[:atom_count][None]
    grad_terms = tuple((term.astype(jnp.float32) for term in pulled[1:]))
    shard_refs = (w_zero, w_one_re, w_one_im, w_two_re, w_two_im, w_target, alpha_vec)
    grand_totals = lax.psum(grad_terms, ("dp", "graph"))
    position = lax.axis_index("graph")
    shards = tuple(
        (
            lax.dynamic_slice_in_dim(
                summed_all, position * shard_ref.shape[0], shard_ref.shape[0], 0
            )
            for summed_all, shard_ref in zip(grand_totals, shard_refs)
        )
    )
    attended = summed.astype(jnp.bfloat16)[None]
    return (
        attended,
        grad_features,
        shards[0],
        shards[1],
        shards[2],
        shards[3],
        shards[4],
        shards[5],
        shards[6],
    )


def solution(mesh):
    in_specs = (
        P("dp", "graph", None),
        P("dp", "graph", None),
        P("dp", None, "graph"),
        P("dp", "graph"),
        P("dp", "graph"),
        P("dp", "graph"),
        P("dp", "graph"),
        P("graph", None),
        P("graph", None),
        P("graph", None),
        P("graph", None),
        P("graph", None),
        P("graph", None),
        P("graph", None),
    )
    out_specs = (
        P("dp", "graph", None),
        P("dp", "graph", None),
        P("graph", None),
        P("graph", None),
        P("graph", None),
        P("graph", None),
        P("graph", None),
        P("graph", None),
        P("graph", None),
    )
    return jax.shard_map(body, mesh=mesh, in_specs=in_specs, out_specs=out_specs, check_vma=False)
```

profile of v0, /device:TPU:0, one launch (start us, length us, event | category | flops | bytes accessed | tf_op | source)
XLA Modules:
  0.0 474.8 jit_solution(5100000157046764141)
XLA Ops:
  11.7 3.4 collective-permute-start.1
  25.2 9.0 %all_gather.23 = bf16[64,8]{1,0:T(8,128)(2,1)S(1)} all-gather(bf16[8,8]{1,0:T(8,128)(2,1)S(1)} %copy-done.539), channel_id=1, replica_groups=mesh['dp'=4,'graph'=8] {'graph'}, dimensions={0}, use_global_device_ids=true | all-gather | bytes 1152 | tf_op jit(solution)/shard_map/all_gather | solution.py:184
  35.0 8.3 %all_gather.22 = bf16[128,512]{1,0:T(8,128)(2,1)S(1)} all-gather(bf16[16,512]{1,0:T(8,128)(2,1)S(1)} %copy-done.528), channel_id=1, replica_groups=mesh['dp'=4,'graph'=8] {'graph'}, dimensions={0}, use_global_device_ids=true | all-gather | bytes 147456 | tf_op jit(solution)/shard_map/all_gather | solution.py:183
  43.4 10.1 %all_gather.26 = bf16[384,192]{1,0:T(8,128)(2,1)} all-gather(bf16[48,192]{1,0:T(8,128)(2,1)S(1)} %copy-done.524), channel_id=1, replica_groups=mesh['dp'=4,'graph'=8] {'graph'}, dimensions={0}, use_global_device_ids=true | all-gather | bytes 165888 | tf_op jit(solution)/shard_map/all_gather | solution.py:181
  53.5 8.4 %all_gather.27 = bf16[384,192]{1,0:T(8,128)(2,1)S(1)} all-gather(bf16[48,192]{1,0:T(8,128)(2,1)S(1)} %copy-done.525), channel_id=1, replica_groups=mesh['dp'=4,'graph'=8] {'graph'}, dimensions={0}, use_global_device_ids=true | all-gather | bytes 165888 | tf_op jit(solution)/shard_map/all_gather | solution.py:182
  61.8 10.2 %all_gather.24 = bf16[512,256]{1,0:T(8,128)(2,1)} all-gather(bf16[64,256]{1,0:T(8,128)(2,1)S(1)} %copy-done.190), channel_id=1, replica_groups=mesh['dp'=4,'graph'=8] {'graph'}, dimensions={0}, use_global_device_ids=true | all-gather | bytes 294912 | tf_op jit(solution)/shard_map/all_gather | solution.py:179
  72.0 9.6 %all_gather.25 = bf16[512,256]{1,0:T(8,128)(2,1)} all-gather(bf16[64,256]{1,0:T(8,128)(2,1)S(1)} %copy-done.191), channel_id=1, replica_groups=mesh['dp'=4,'graph'=8] {'graph'}, dimensions={0}, use_global_device_ids=true | all-gather | bytes 294912 | tf_op jit(solution)/shard_map/all_gather | solution.py:180
  86.1 1.8 gather_fusion.5
  93.0 1.3 pad_maximum_fusion.9
  103.0 2.0 gather_fusion.4
  105.2 1.7 copy_select_fusion
  109.9 1.4 constant_dynamic-update-slice_fusion.4
  113.1 1.6 multiply_add_fusion.14
  114.7 1.6 constant_dynamic-update-slice_fusion.2
  126.2 1.8 fusion.145
  140.2 1.6 slice_multiply_fusion
  142.0 1.3 scatter_custom_fusion
  146.0 2.4 scatter_custom_fusion.1
  149.1 1.6 fusion.17
  152.9 2.3 fusion.126
  155.2 1.8 reshape.3774
  157.0 2.3 fusion.127
  162.1 1.4 fusion.3
  163.4 1.3 copy.189
  165.6 1.6 copy.223
  167.2 2.0 fusion.11
  169.2 1.9 fusion.9
  180.6 1.9 slice_multiply_fusion.116
  185.9 1.9 slice_multiply_fusion.49
  193.6 1.7 slice_multiply_fusion.25
  195.3 1.9 slice_multiply_fusion.30
  198.6 1.9 fusion.2
  203.8 40.2 %psum.55 = f32[64,8]{1,0:T(8,128)} all-reduce(f32[64,8]{1,0:T(8,128)S(1)} %convert_bitcast_fusion), channel_id=1, replica_groups=mesh['dp'=4,'graph'=8] {'dp','graph'}, use_global_device_ids=true, to_apply=%region_30.32 | all-reduce | flops 512 | bytes 4096 | tf_op jit(solution)/shard_map/psum | solution.py:229
  245.2 2.1 scatter_custom_fusion.6
  247.4 2.0 fusion.7
  267.4 2.0 pad_add_fusion
  271.1 1.9 pad_add_fusion.4
  274.3 13.1 %scatter_fusion.3 = f32[32,3,128]{2,1,0:T(4,128)S(1)} fusion(f32[32,3,128]{2,1,0:T(4,128)S(1)} %broadcast_in_dim.136, s32[192]{0:T(256)S(1)} %bitcast.473, f32[192,3,128]{2,1,0:T(4,128)} %copy.207), kind=kCustom, calls=%fused_computation.14 | custom fusion | flops 73728 | bytes 885504 | tf_op jit(solution)/shard_map/transpose(jvp(jit(_take)))/scatter-add | solution.py:86
  287.4 7.6 %scatter_fusion = f32[32,9,128]{2,1,0:T(8,128)S(1)} fusion(f32[32,9,128]{2,1,0:T(8,128)S(1)} %broadcast_in_dim.133, s32[192]{0:T(256)S(1)} %bitcast.474, f32[192,9,128]{2,1,0:T(8,128)S(1)} %copy.191), kind=kCustom, calls=%fused_computation.11 | custom fusion | flops 221184 | bytes 2654976 | tf_op jit(solution)/shard_map/transpose(jvp(jit(_take)))/scatter-add | solution.py:86
  295.1 7.2 %scatter_fusion.1 = f32[32,7,128]{2,1,0:T(8,128)S(1)} fusion(f32[32,7,128]{2,1,0:T(8,128)S(1)} %broadcast_in_dim.134, s32[192]{0:T(256)S(1)} %bitcast.475, f32[192,7,128]{2,1,0:T(8,128)S(1)} %copy.197), kind=kCustom, calls=%fused_computation.12 | custom fusion | flops 172032 | bytes 2065152 | tf_op jit(solution)/shard_map/transpose(jvp(jit(_take)))/scatter-add | solution.py:86
  302.3 7.2 %scatter_fusion.2 = f32[32,5,128]{2,1,0:T(8,128)S(1)} fusion(f32[32,5,128]{2,1,0:T(8,128)S(1)} %broadcast_in_dim.135, s32[192]{0:T(256)S(1)} %bitcast.476, f32[192,5,128]{2,1,0:T(8,128)S(1)} %copy.203), kind=kCustom, calls=%fused_computation.13 | custom fusion | flops 122880 | bytes 1475328 | tf_op jit(solution)/shard_map/transpose(jvp(jit(_take)))/scatter-add | solution.py:86
  310.0 2.6 collective-permute-start.3
  317.7 140.8 %all-reduce.276.cloned.1.call-done = (f32[640,832]{1,0:T(8,128)}, f32[512,256]{1,0:T(8,128)}, f32[512,256]{1,0:T(8,128)}, f32[384,192]{1,0:T(8,128)}, f32[384,192]{1,0:T(8,128)}, /*index=5*/f32[128,512]{0,1:T(8,128)}) async-done(((f32[640,832]{1,0:T(8,128)}, f32[512,256]{1,0:T(8,128)}, f32[512,256]{1,0:T(8,128)}, f32[384,192]{1,0:T(8,128)}, f32[384,192]{1,0:T(8,128)}, /*index=5*/f32[128,512]{0,1:T(8,128)}), ...) | async-done | bytes 4030480 | tf_op jit(solution)/shard_map/psum | solution.py:229
  458.5 1.4 constant_dynamic-slice_fusion.3
  459.9 1.4 constant_dynamic-slice_fusion.2
  461.3 1.5 constant_dynamic-slice_fusion.5
  462.8 1.5 constant_dynamic-slice_fusion.4
  466.1 1.7 constant_dynamic-slice_fusion.6
  (1325 shorter events, 115.4 us)
Async XLA Ops:
  7.2 74.6 %copy-start = (f32[1,16,1600]{2,1,0:T(8,128)S(1)}, f32[1,16,1600]{2,1,0:T(8,128)}, u32[]{:S(2)}) copy-start(f32[1,16,1600]{2,1,0:T(8,128)} %param.17) | copy-start | bytes 307204
  7.2 9.7 %copy-start.541 = (s32[1,8]{1,0:T(1,128)S(1)}, s32[1,8]{1,0:T(1,128)}, u32[]{:S(2)}) copy-start(s32[1,8]{1,0:T(1,128)} %param.20) | copy-start | bytes 100
  7.2 9.2 %copy-start.540 = (s32[1,8]{1,0:T(1,128)S(1)}, s32[1,8]{1,0:T(1,128)}, u32[]{:S(2)}) copy-start(s32[1,8]{1,0:T(1,128)} %param.19) | copy-start | bytes 100
  7.2 10.3 %copy-start.30 = (bf16[1,114,192]{1,2,0:T(8,128)(2,1)S(1)}, bf16[1,114,192]{1,2,0:T(8,128)(2,1)}, u32[]{:S(2)}) copy-start(bf16[1,114,192]{1,2,0:T(8,128)(2,1)} %param.18) | copy-start | bytes 131332
  7.2 119.0 %all-gather.2.cloned.1.call-start = ((), (), s32[]{:S(2)}) async-start(), calls=%async_computation | async-start | bytes 1290240 | tf_op jit(solution)/shard_map/all_gather | solution.py:178
  8.0 450.5 %all-reduce.276.cloned.1.call-start = ((), (), s32[]{:S(2)}) async-start(), calls=%async_computation.1 | async-start | bytes 8781824 | tf_op jit(solution)/shard_map/psum | solution.py:229
  10.3 12.3 %copy-start.25 = (f32[1,16,3200]{2,1,0:T(8,128)S(1)}, f32[1,16,3200]{2,1,0:T(8,128)}, u32[]{:S(2)}) copy-start(f32[1,16,3200]{2,1,0:T(8,128)} %param.16) | copy-start | bytes 614404
  10.3 12.4 %copy-start.542 = (s32[1,192]{1,0:T(1,128)S(1)}, s32[1,192]{1,0:T(1,128)}, u32[]{:S(2)}) copy-start(s32[1,192]{1,0:T(1,128)} %param.21) | copy-start | bytes 2308
  10.3 12.9 %copy-start.531 = (s32[1,192]{1,0:T(1,128)S(1)}, s32[1,192]{1,0:T(1,128)}, u32[]{:S(2)}) copy-start(s32[1,192]{1,0:T(1,128)} %param.22) | copy-start | bytes 2308
  11.0 14.3 %copy-start.539 = (bf16[8,8]{1,0:T(8,128)(2,1)S(1)}, bf16[8,8]{1,0:T(8,128)(2,1)}, u32[]{:S(2)}) copy-start(bf16[8,8]{1,0:T(8,128)(2,1)} %param.29) | copy-start | bytes 388
  11.0 24.0 %copy-start.528 = (bf16[16,512]{1,0:T(8,128)(2,1)S(1)}, bf16[16,512]{1,0:T(8,128)(2,1)}, u32[]{:S(2)}) copy-start(bf16[16,512]{1,0:T(8,128)(2,1)} %param.28) | copy-start | bytes 49156
  11.0 32.4 %copy-start.524 = (bf16[48,192]{1,0:T(8,128)(2,1)S(1)}, bf16[48,192]{1,0:T(8,128)(2,1)}, u32[]{:S(2)}) copy-start(bf16[48,192]{1,0:T(8,128)(2,1)} %param.26) | copy-start | bytes 55300
  11.7 80.6 %collective-permute-start.1 = (f32[8,3200]{1,0:T(8,128)}, f32[8,3200]{1,0:T(8,128)}, u32[]{:S(2)}, u32[]{:S(2)}) collective-permute-start(f32[8,3200]{1,0:T(8,128)} %broadcast_select_fusion), channel_id=1, source_target_pairs={{1,0},{2,1},{3,2},{4,3},{5,4},{6,5},{7,6},{0,7},{9,8},{10,9},{11,1... | collective-permute-start | bytes 307208 | tf_op jit(solution)/shard_map/ppermute | solution.py:18
  15.1 38.4 %copy-start.525 = (bf16[48,192]{1,0:T(8,128)(2,1)S(1)}, bf16[48,192]{1,0:T(8,128)(2,1)}, u32[]{:S(2)}) copy-start(bf16[48,192]{1,0:T(8,128)(2,1)} %param.27) | copy-start | bytes 55300
  15.1 46.8 %copy-start.190 = (bf16[64,256]{1,0:T(8,128)(2,1)S(1)}, bf16[64,256]{1,0:T(8,128)(2,1)}, u32[]{:S(2)}) copy-start(bf16[64,256]{1,0:T(8,128)(2,1)} %param.24) | copy-start | bytes 98308
  15.7 56.3 %copy-start.191 = (bf16[64,256]{1,0:T(8,128)(2,1)S(1)}, bf16[64,256]{1,0:T(8,128)(2,1)}, u32[]{:S(2)}) copy-start(bf16[64,256]{1,0:T(8,128)(2,1)} %param.25) | copy-start | bytes 98308
  16.4 75.9 %collective-permute-start = (f32[8,3200]{1,0:T(8,128)}, f32[8,3200]{1,0:T(8,128)}, u32[]{:S(2)}, u32[]{:S(2)}) collective-permute-start(f32[8,3200]{1,0:T(8,128)} %broadcast_select_fusion.1), channel_id=1, source_target_pairs={{0,1},{1,2},{2,3},{3,4},{4,5},{5,6},{6,7},{7,0},{8,9},{9,10},{10,1... | collective-permute-start | bytes 307208 | tf_op jit(solution)/shard_map/ppermute | solution.py:15
  18.3 80.5 %copy-start.195 = (f32[1,1,192]{2,1,0:T(1,128)}, f32[1,1,192]{2,1,0:T(1,128)S(1)}, u32[]{:S(2)}) copy-start(f32[1,1,192]{2,1,0:T(1,128)S(1)} %get-tuple-element.450) | copy-start | bytes 2308
  18.3 80.5 %copy-start.201 = (f32[1,1,192]{2,1,0:T(1,128)}, f32[1,1,192]{2,1,0:T(1,128)S(1)}, u32[]{:S(2)}) copy-start(f32[1,1,192]{2,1,0:T(1,128)S(1)} %get-tuple-element.451) | copy-start | bytes 2308
  18.3 80.5 %copy-start.207 = (f32[1,1,192]{2,1,0:T(1,128)}, f32[1,1,192]{2,1,0:T(1,128)S(1)}, u32[]{:S(2)}) copy-start(f32[1,1,192]{2,1,0:T(1,128)S(1)} %get-tuple-element.452) | copy-start | bytes 2308
  18.3 98.0 %copy-start.192 = (f32[1,1,192]{2,1,0:T(1,128)}, f32[1,1,192]{2,1,0:T(1,128)S(1)}, u32[]{:S(2)}) copy-start(f32[1,1,192]{2,1,0:T(1,128)S(1)} %get-tuple-element.455) | copy-start | bytes 2308
  18.3 98.0 %copy-start.198 = (f32[1,1,192]{2,1,0:T(1,128)}, f32[1,1,192]{2,1,0:T(1,128)S(1)}, u32[]{:S(2)}) copy-start(f32[1,1,192]{2,1,0:T(1,128)S(1)} %get-tuple-element.456) | copy-start | bytes 2308
  18.4 98.0 %copy-start.204 = (f32[1,1,192]{2,1,0:T(1,128)}, f32[1,1,192]{2,1,0:T(1,128)S(1)}, u32[]{:S(2)}) copy-start(f32[1,1,192]{2,1,0:T(1,128)S(1)} %get-tuple-element.457) | copy-start | bytes 2308
  23.3 10.9 %copy-start.538 = (s32[192,1]{0,1:T(1,128)}, s32[192,1]{0,1:T(1,128)S(1)}, u32[]{:S(2)}) copy-start(s32[192,1]{0,1:T(1,128)S(1)} %get-tuple-element.471) | copy-start | bytes 2308
  23.3 68.9 %copy-start.188 = (s32[192,1]{0,1:T(1,128)}, s32[192,1]{0,1:T(1,128)S(1)}, u32[]{:S(2)}) copy-start(s32[192,1]{0,1:T(1,128)S(1)} %get-tuple-element.472) | copy-start | bytes 2308
  43.2 38.5 %copy-start.23 = (bf16[128,512]{1,0:T(8,128)(2,1)}, bf16[128,512]{1,0:T(8,128)(2,1)S(1)}, u32[]{:S(2)}) copy-start(bf16[128,512]{1,0:T(8,128)(2,1)S(1)} %all_gather.22) | copy-start | bytes 393220
  92.3 10.7 %copy-start.526 = (s32[1024]{0:T(1024)}, s32[1024]{0:T(1024)S(1)}, u32[]{:S(2)}) copy-start(s32[1024]{0:T(1024)S(1)} %pad_clamp_fusion.1) | copy-start | bytes 12292
  102.8 22.4 %copy-start.58 = (bf16[192,1,128]{2,0,1:T(8,128)(2,1)}, bf16[192,1,128]{2,0,1:T(8,128)(2,1)S(1)}, u32[]{:S(2)}) copy-start(bf16[192,1,128]{2,0,1:T(8,128)(2,1)S(1)} %multiply_add_fusion.6) | copy-start | bytes 147460
  128.2 12.0 %copy-start.4 = (f32[192,320]{0,1:T(8,128)}, f32[192,320]{0,1:T(8,128)S(1)}, u32[]{:S(2)}) copy-start(f32[192,320]{0,1:T(8,128)S(1)} %copy.171) | copy-start | bytes 737284
  128.9 15.7 %copy-start.161 = (f32[192,8]{0,1:T(8,128)}, f32[192,8]{0,1:T(8,128)S(1)}, u32[]{:S(2)}) copy-start(f32[192,8]{0,1:T(8,128)S(1)} %fusion.106) | copy-start | bytes 18436
  152.9 9.2 %copy-start.3 = (bf16[640,832]{1,0:T(8,128)(2,1)S(1)}, bf16[640,832]{1,0:T(8,128)(2,1)}, u32[]{:S(2)}) copy-start(bf16[640,832]{1,0:T(8,128)(2,1)} %all-gather.2.cloned.1.call-done) | copy-start | bytes 3194884
  202.9 41.1 %copy-start.163 = (bf16[192,4,64]{0,2,1:T(8,128)(2,1)S(1)}, bf16[192,4,64]{0,2,1:T(8,128)(2,1)}, u32[]{:S(2)}) copy-start(bf16[192,4,64]{0,2,1:T(8,128)(2,1)} %get-tuple-element.64) | copy-start | bytes 294916
  202.9 41.1 %copy-start.169 = (bf16[192,1,128]{2,0,1:T(8,128)(2,1)S(1)}, bf16[192,1,128]{2,0,1:T(8,128)(2,1)}, u32[]{:S(2)}) copy-start(bf16[192,1,128]{2,0,1:T(8,128)(2,1)} %multiply_add_fusion.11) | copy-start | bytes 147460
  202.9 41.1 %copy-start.174 = (bf16[192,1,128]{2,0,1:T(8,128)(2,1)S(1)}, bf16[192,1,128]{2,0,1:T(8,128)(2,1)}, u32[]{:S(2)}) copy-start(bf16[192,1,128]{2,0,1:T(8,128)(2,1)} %multiply_add_fusion.12) | copy-start | bytes 147460
  202.9 41.1 %copy-start.179 = (bf16[192,1,128]{2,0,1:T(8,128)(2,1)S(1)}, bf16[192,1,128]{2,0,1:T(8,128)(2,1)}, u32[]{:S(2)}) copy-start(bf16[192,1,128]{2,0,1:T(8,128)(2,1)} %multiply_add_fusion.13) | copy-start | bytes 147460
  202.9 41.1 %copy-start.184 = (bf16[192,1,128]{2,0,1:T(8,128)(2,1)S(1)}, bf16[192,1,128]{2,0,1:T(8,128)(2,1)}, u32[]{:S(2)}) copy-start(bf16[192,1,128]{2,0,1:T(8,128)(2,1)} %copy-done.183) | copy-start | bytes 147460
  202.9 42.1 %copy-start.50 = (f32[192,1,128]{0,2,1:T(8,128)S(1)}, f32[192,1,128]{0,2,1:T(8,128)}, u32[]{:S(2)}) copy-start(f32[192,1,128]{0,2,1:T(8,128)} %get-tuple-element.185) | copy-start | bytes 294916
  202.9 42.2 %copy-start.49 = (f32[192,1,128]{0,2,1:T(8,128)S(1)}, f32[192,1,128]{0,2,1:T(8,128)}, u32[]{:S(2)}) copy-start(f32[192,1,128]{0,2,1:T(8,128)} %get-tuple-element.188) | copy-start | bytes 294916
  202.9 44.4 %copy-start.172 = (bf16[192,1,128]{2,0,1:T(8,128)(2,1)S(1)}, bf16[192,1,128]{2,0,1:T(8,128)(2,1)}, u32[]{:S(2)}) copy-start(bf16[192,1,128]{2,0,1:T(8,128)(2,1)} %multiply_add_fusion.7) | copy-start | bytes 147460
  202.9 44.4 %copy-start.177 = (bf16[192,1,128]{2,0,1:T(8,128)(2,1)S(1)}, bf16[192,1,128]{2,0,1:T(8,128)(2,1)}, u32[]{:S(2)}) copy-start(bf16[192,1,128]{2,0,1:T(8,128)(2,1)} %multiply_add_fusion.8) | copy-start | bytes 147460
  202.9 44.4 %copy-start.182 = (bf16[192,1,128]{2,0,1:T(8,128)(2,1)S(1)}, bf16[192,1,128]{2,0,1:T(8,128)(2,1)}, u32[]{:S(2)}) copy-start(bf16[192,1,128]{2,0,1:T(8,128)(2,1)} %multiply_add_fusion.9) | copy-start | bytes 147460
  203.0 44.4 %copy-start.187 = (bf16[192,1,128]{2,0,1:T(8,128)(2,1)S(1)}, bf16[192,1,128]{2,0,1:T(8,128)(2,1)}, u32[]{:S(2)}) copy-start(bf16[192,1,128]{2,0,1:T(8,128)(2,1)} %copy-done.185) | copy-start | bytes 147460
  203.6 45.8 %copy-start.545 = (bf16[512,256]{1,0:T(8,128)(2,1)S(1)}, bf16[512,256]{1,0:T(8,128)(2,1)}, u32[]{:S(2)}) copy-start(bf16[512,256]{1,0:T(8,128)(2,1)} %convolution_convert_fusion.5) | copy-start | bytes 786436
  258.8 8.2 %copy-start.151 = (f32[192,1,128]{2,0,1:T(8,128)S(1)}, f32[192,1,128]{2,0,1:T(8,128)}, u32[]{:S(2)}) copy-start(f32[192,1,128]{2,0,1:T(8,128)} %get-tuple-element.191) | copy-start | bytes 294916
  258.8 8.2 %copy-start.152 = (f32[192,1,128]{2,0,1:T(8,128)S(1)}, f32[192,1,128]{2,0,1:T(8,128)}, u32[]{:S(2)}) copy-start(f32[192,1,128]{2,0,1:T(8,128)} %get-tuple-element.192) | copy-start | bytes 294916
  309.9 5.1 %collective-permute-start.2 = (bf16[8,3200]{1,0:T(8,128)(2,1)S(1)}, bf16[8,3200]{1,0:T(8,128)(2,1)S(1)}, u32[]{:S(2)}, u32[]{:S(2)}) collective-permute-start(bf16[8,3200]{1,0:T(8,128)(2,1)S(1)} %get-tuple-element.340), channel_id=1, source_target_pairs={{0,1},{1,2},{2,3},{3,4},{4,5},{5,6},{6,7},{7,0},{8,9},{9,10},{10,1... | collective-permute-start | bytes 153608 | tf_op jit(solution)/shard_map/ppermute | solution.py:15
  310.0 5.0 %collective-permute-start.3 = (bf16[8,3200]{1,0:T(8,128)(2,1)S(1)}, bf16[8,3200]{1,0:T(8,128)(2,1)S(1)}, u32[]{:S(2)}, u32[]{:S(2)}) collective-permute-start(bf16[8,3200]{1,0:T(8,128)(2,1)S(1)} %get-tuple-element.341), channel_id=1, source_target_pairs={{1,0},{2,1},{3,2},{4,3},{5,4},{6,5},{7,6},{0,7},{9,8},{10,9},{11,1... | collective-permute-start | bytes 153608 | tf_op jit(solution)/shard_map/ppermute | solution.py:18
  315.0 152.7 %copy-start.1 = (f32[1,16,1600]{2,1,0:T(8,128)S(1)}, f32[1,16,1600]{2,1,0:T(8,128)}, u32[]{:S(2)}) copy-start(f32[1,16,1600]{2,1,0:T(8,128)} %param.17) | copy-start | bytes 307204
  (504 other events, 1758.2 us)
Sparse Core Ops, SparseCore 0:
  9.9 26.5 all-gather.1
  312.8 145.6 all-reduce.275
where the time goes:
time: 482 us; the launch traced here: 475 us
  waiting for transfers between devices  141 us (29%)
  other arithmetic  119 us (25%)
  blocking collectives  95.7 us (20%)
  local copies, waits for them, and re-layouts  58.4 us (12%)
  matrix products  31.6 us (7%)
  between operations  22.3 us (5%)
  starting transfers between devices  6.1 us (1%)
    psum x1, waiting for transfers between devices, body(): grand_totals = lax.psum(grad_terms, ('dp', 'graph'))  141 us
    psum x1, blocking collectives, body(): grand_totals = lax.psum(grad_terms, ('dp', 'graph'))  40.2 us
    scatter-add x4, other arithmetic, attend(): jnp.take(coeffs[:, degree * degree:(degree + 1) * (degree + 1), :], edge_...  35.1 us
    mul x13, other arithmetic, apply_block(): total = total + block[row, column][:, None] * source_part[:, column, :]  17.5 us
    unnamed x26, other arithmetic  15.7 us
    all_gather x1, blocking collectives, body(): lax.all_gather(w_one_re, 'graph', axis=0, tiled=True)  10.2 us
    all_gather x1, blocking collectives, body(): lax.all_gather(w_two_re, 'graph', axis=0, tiled=True)  10.1 us
    dynamic_slice x7, local copies, waits for them, and re-layouts, body(): lax.dynamic_slice_in_dim(summed_all, position * shard_ref.shape[0], shard...  9.83 us
  transfers between devices with their start and end apart: 6, of which 1 were waited for; matrix products, arithmetic and copies ran while one was open for 13% of the time, Pallas kernels for 0%

commit v1 on v0

v1 whole, which is shorter than its diff:
```python
from functools import partial

import jax
import jax.numpy as jnp
from jax import lax
from jax.experimental import pallas as pl
from jax.experimental.pallas import tpu as pltpu
from jax.sharding import PartitionSpec as P

F32 = jnp.float32
BF16 = jnp.bfloat16
OFFSETS = {1: 0, 2: 9, 3: 34, 4: 69}
DEGREES = (1, 2, 3, 4)
BLOCK_C = 32
BLOCK_H = 16


def slot(degree, azimuth):
    return {0: degree, 1: 4 + degree, -1: 8 + degree, 2: 11 + degree, -2: 14 + degree}[azimuth]


def orders(degree):
    kept = min(degree, 2)
    return range(-kept, kept + 1)


def rot_row(degree, azimuth, column):
    return OFFSETS[degree] + (azimuth + min(degree, 2)) * (2 * degree + 1) + column


def dot(a, b, ca, cb, precision=None):
    return lax.dot_general(
        a, b, (((ca,), (cb,)), ((), ())), preferred_element_type=F32, precision=precision
    )


def compute_kernel(
    ext_ref, cot_ref, rotation_ref, src_ref, tgt_ref,
    wz_ref, w1r_ref, w1i_ref, w2r_ref, w2i_ref, wt_ref, alpha_ref,
    att_ref, own_ref, ghost_ref, gz_ref, g1r_ref, g1i_ref, g2r_ref, g2i_ref, gt_ref, ga_ref,
    rotf, xs, turned, hid, msg, dmsg, scores, dhid, dmixed, dturned, dxs, small, spreads,
):
    edges = rotation_ref.shape[1]
    rows = ext_ref.shape[0]
    atoms = att_ref.shape[0]
    channels = wt_ref.shape[0]
    hidden = w1r_ref.shape[1] // 4
    heads = small.shape[1]
    width = alpha_ref.shape[0] // heads

    rotf[...] = rotation_ref[...].astype(F32)
    src_hot = (
        lax.broadcasted_iota(jnp.int32, (rows, edges), 0) == src_ref[...]
    ).astype(F32).astype(BF16)
    member = (lax.broadcasted_iota(jnp.int32, (atoms, edges), 0) == tgt_ref[...]).astype(F32)
    member_b = member.astype(BF16)

    for k in range(25):
        xs[k] = dot(ext_ref[:, k * channels:(k + 1) * channels], src_hot, 0, 0)
        dmsg[k] = dot(
            cot_ref[:, k * hidden:(k + 1) * hidden].astype(BF16), member_b, 0, 0
        )

    def turn(i, carry):
        part = pl.ds(pl.multiple_of(i * BLOCK_C, BLOCK_C), BLOCK_C)
        turned[0, part, :] = xs[0, part, :].astype(BF16)
        for degree in DEGREES:
            for azimuth in orders(degree):
                total = None
                for n in range(2 * degree + 1):
                    k = rot_row(degree, azimuth, n)
                    term = rotf[k:k + 1, :] * xs[degree * degree + n, part, :]
                    total = term if total is None else total + term
                turned[slot(degree, azimuth), part, :] = total.astype(BF16)
        return carry

    lax.fori_loop(0, channels // BLOCK_C, turn, 0)

    zero_in = turned[0:5].reshape(5 * channels, edges)
    one_pos = turned[5:9].reshape(4 * channels, edges)
    one_neg = turned[9:13].reshape(4 * channels, edges)
    two_pos = turned[13:16].reshape(3 * channels, edges)
    two_neg = turned[16:19].reshape(3 * channels, edges)

    hid[0:5] = dot(wz_ref[:, :5 * hidden], zero_in, 0, 0).reshape(5, hidden, edges)
    per_atom = dot(ext_ref[:atoms, :channels], wt_ref[...], 1, 0)
    high = per_atom.astype(BF16)
    low = (per_atom - high.astype(F32)).astype(BF16)
    scores[...] = (
        dot(wz_ref[:, 5 * hidden:], zero_in, 0, 0)
        + dot(high, member_b, 0, 0)
        + dot(low, member_b, 0, 0)
    )
    hid[5:9] = (dot(w1r_ref[...], one_pos, 0, 0) - dot(w1i_ref[...], one_neg, 0, 0)).reshape(
        4, hidden, edges)
    hid[9:13] = (dot(w1r_ref[...], one_neg, 0, 0) + dot(w1i_ref[...], one_pos, 0, 0)).reshape(
        4, hidden, edges)
    hid[13:16] = (dot(w2r_ref[...], two_pos, 0, 0) - dot(w2i_ref[...], two_neg, 0, 0)).reshape(
        3, hidden, edges)
    hid[16:19] = (dot(w2r_ref[...], two_neg, 0, 0) + dot(w2i_ref[...], two_pos, 0, 0)).reshape(
        3, hidden, edges)

    for h in range(heads):
        part = slice(h * width, (h + 1) * width)
        value = scores[part, :]
        centre = value - jnp.mean(value, axis=0, keepdims=True)
        scale = lax.rsqrt(jnp.mean(centre * centre, axis=0, keepdims=True) + 1e-05)
        normed = centre * scale
        scores[part, :] = normed
        gate = 0.2 + 0.8 * jax.nn.sigmoid(normed)
        small[0, h:h + 1, :] = jnp.sum(
            normed * gate * alpha_ref[part, :], axis=0, keepdims=True
        )
        small[1, h:h + 1, :] = scale

    exact = lax.Precision.HIGHEST
    raised = jnp.exp(small[0])
    totals = dot(dot(raised, member, 1, 1, exact), member, 1, 0, exact)
    weights = raised / totals
    spreads[0] = jnp.broadcast_to(
        weights[:, None, :], (heads, hidden // heads, edges)
    ).reshape(hidden, edges)

    def mix(i, carry):
        part = pl.ds(pl.multiple_of(i * BLOCK_H, BLOCK_H), BLOCK_H)
        spread = spreads[0, part, :]
        scalar = hid[0, part, :]
        gating = jax.nn.sigmoid(scalar)
        silu = scalar * gating
        both = gating * spread
        msg[0, part, :] = (silu * spread).astype(BF16)
        d_first = dmsg[0, part, :]
        inner = jnp.zeros_like(scalar)
        for degree in DEGREES:
            size = 2 * degree + 1
            sums = [None] * size
            for azimuth in orders(degree):
                raw = hid[slot(degree, azimuth), part, :]
                value = raw * both
                back = None
                for n in range(size):
                    k = rot_row(degree, azimuth, n)
                    line = rotf[k:k + 1, :]
                    term = line * value
                    sums[n] = term if sums[n] is None else sums[n] + term
                    other = line * dmsg[degree * degree + n, part, :]
                    back = other if back is None else back + other
                inner = inner + back * raw
                dhid[slot(degree, azimuth), part, :] = (back * both).astype(BF16)
            for n in range(size):
                msg[degree * degree + n, part, :] = sums[n].astype(BF16)
        spreads[1, part, :] = inner * gating + d_first * silu
        d_scalar = d_first * spread * gating * (1.0 + scalar * (1.0 - gating)) + (
            inner * spread * gating * (1.0 - gating)
        )
        dhid[0, part, :] = d_scalar.astype(BF16)
        return carry

    lax.fori_loop(0, hidden // BLOCK_H, mix, 0)

    att_ref[...] = dot(member_b, msg[...].reshape(25 * hidden, edges), 1, 1).astype(BF16)

    d_weights = jnp.sum(
        spreads[1].reshape(heads, hidden // heads, edges), axis=1
    )
    product = weights * d_weights
    d_logits = product - weights * dot(
        dot(product, member, 1, 1, exact), member, 1, 0, exact
    )
    small[0] = d_logits
    for h in range(heads):
        part = slice(h * width, (h + 1) * width)
        normed = scores[part, :]
        sig = jax.nn.sigmoid(normed)
        gate = 0.2 + 0.8 * sig
        d_logit = small[0, h:h + 1, :]
        ga_ref[part, :] = jnp.sum(normed * gate * d_logit, axis=1, keepdims=True)
        d_norm = d_logit * alpha_ref[part, :] * (gate + 0.8 * normed * sig * (1.0 - sig))
        first = jnp.mean(d_norm, axis=0, keepdims=True)
        second = jnp.mean(d_norm * normed, axis=0, keepdims=True)
        d_score = small[1, h:h + 1, :] * (d_norm - first - normed * second)
        dmixed[5 * hidden + h * width:5 * hidden + (h + 1) * width, :] = d_score.astype(BF16)
    dmixed[:5 * hidden, :] = dhid[0:5].reshape(5 * hidden, edges)

    d_per_atom = dot(member_b, dmixed[5 * hidden:, :], 1, 1).astype(BF16)
    gt_ref[...] = dot(ext_ref[:atoms, :channels], d_per_atom, 0, 0).astype(BF16)
    d_target = dot(d_per_atom, wt_ref[...], 1, 1)

    gz_ref[...] = dot(zero_in, dmixed[...], 1, 1).astype(BF16)
    dturned[0:5] = dot(wz_ref[...], dmixed[...], 1, 0).reshape(5, channels, edges)

    def pair(first, count, re_ref, im_ref, gre_ref, gim_ref, pos, neg):
        middle = first + count
        last = middle + count
        up = dhid[first:middle].reshape(count * hidden, edges)
        down = dhid[middle:last].reshape(count * hidden, edges)
        gre_ref[...] = (dot(pos, up, 1, 1) + dot(neg, down, 1, 1)).astype(BF16)
        gim_ref[...] = (dot(pos, down, 1, 1) - dot(neg, up, 1, 1)).astype(BF16)
        dturned[first:middle] = (
            dot(re_ref[...], up, 1, 0) + dot(im_ref[...], down, 1, 0)
        ).reshape(count, channels, edges)
        dturned[middle:last] = (
            dot(re_ref[...], down, 1, 0) - dot(im_ref[...], up, 1, 0)
        ).reshape(count, channels, edges)

    pair(5, 4, w1r_ref, w1i_ref, g1r_ref, g1i_ref, one_pos, one_neg)
    pair(13, 3, w2r_ref, w2i_ref, g2r_ref, g2i_ref, two_pos, two_neg)

    def turn_back(i, carry):
        part = pl.ds(pl.multiple_of(i * BLOCK_C, BLOCK_C), BLOCK_C)
        dxs[0, part, :] = dturned[0, part, :].astype(BF16)
        for degree in DEGREES:
            for n in range(2 * degree + 1):
                total = None
                for azimuth in orders(degree):
                    k = rot_row(degree, azimuth, n)
                    term = rotf[k:k + 1, :] * dturned[slot(degree, azimuth), part, :]
                    total = term if total is None else total + term
                dxs[degree * degree + n, part, :] = total.astype(BF16)
        return carry

    lax.fori_loop(0, channels // BLOCK_C, turn_back, 0)

    ext_grad = dot(src_hot, dxs[...].reshape(25 * channels, edges), 1, 1)
    own_ref[...] = ext_grad[:atoms]
    own_ref[:, :channels] = ext_grad[:atoms, :channels] + d_target
    ghost_ref[...] = ext_grad[atoms:].astype(BF16)


def compute(ext, cot, rotation, src, tgt, wz, w1r, w1i, w2r, w2i, wt, alpha_col, heads):
    edges = rotation.shape[1]
    atoms = cot.shape[0]
    ghosts = ext.shape[0] - atoms
    channels = wt.shape[0]
    hidden = w1r.shape[1] // 4
    shape = jax.ShapeDtypeStruct
    vmem = pl.BlockSpec(memory_space=pltpu.VMEM)
    out_shape = (
        shape((atoms, 25 * hidden), BF16),
        shape((atoms, 25 * channels), F32),
        shape((ghosts, 25 * channels), BF16),
        shape(wz.shape, BF16),
        shape(w1r.shape, BF16),
        shape(w1i.shape, BF16),
        shape(w2r.shape, BF16),
        shape(w2i.shape, BF16),
        shape(wt.shape, BF16),
        shape(alpha_col.shape, F32),
    )
    scratch = [
        pltpu.VMEM(rotation.shape, F32),
        pltpu.VMEM((25, channels, edges), F32),
        pltpu.VMEM((19, channels, edges), BF16),
        pltpu.VMEM((19, hidden, edges), F32),
        pltpu.VMEM((25, hidden, edges), BF16),
        pltpu.VMEM((25, hidden, edges), F32),
        pltpu.VMEM((alpha_col.shape[0], edges), F32),
        pltpu.VMEM((19, hidden, edges), BF16),
        pltpu.VMEM((wz.shape[1], edges), BF16),
        pltpu.VMEM((19, channels, edges), F32),
        pltpu.VMEM((25, channels, edges), BF16),
        pltpu.VMEM((2, heads, edges), F32),
        pltpu.VMEM((2, hidden, edges), F32),
    ]
    return pl.pallas_call(
        compute_kernel,
        out_shape=out_shape,
        in_specs=[vmem] * 12,
        out_specs=[vmem] * 10,
        scratch_shapes=scratch,
        compiler_params=pltpu.CompilerParams(vmem_limit_bytes=56 * 2**20),
        name="slab",
    )(ext, cot, rotation, src, tgt, wz, w1r, w1i, w2r, w2i, wt, alpha_col)


MESH = pl.DeviceIdType.MESH


def greet(n, depth):
    me = lax.axis_index("graph")
    row = lax.axis_index("dp")
    barrier = pltpu.get_barrier_semaphore()
    for d in range(1, n):
        pl.semaphore_signal(
            barrier, inc=1, device_id=(row, lax.rem(me + d, n)), device_id_type=MESH)
    for d in range(1, depth):
        pl.semaphore_signal(
            barrier, inc=1, device_id=(lax.rem(row + d, depth), me), device_id_type=MESH)
    pl.semaphore_wait(barrier, n - 1 + depth - 1)


def gather_kernel(n, count, *refs):
    shards = refs[:count]
    outgoing = refs[count]
    full = refs[count + 1:2 * count + 1]
    ghosts = refs[2 * count + 1]
    send_sem, recv_sem, pass_sem, local_sem, side_send, side_recv = refs[2 * count + 2:]
    me = lax.axis_index("graph")
    row = lax.axis_index("dp")
    half = n // 2
    sibling = me + 1 - 2 * lax.rem(me, 2)
    right, left = lax.rem(me + 1, n), lax.rem(me + n - 1, n)
    greet(n, 1)

    def remote(src, dst, send, recv, target):
        copy = pltpu.make_async_remote_copy(
            src_ref=src, dst_ref=dst, send_sem=send, recv_sem=recv,
            device_id=(row, target), device_id_type=MESH)
        copy.start()
        return copy

    sends = []
    for side, target in ((1, left), (0, right)):
        sends.append(remote(outgoing.at[1 - side], ghosts.at[side], side_send.at[side],
                            side_recv.at[side], target))
    direct = []
    for d in range(1, half):
        target = lax.rem(me + 2 * d, n)
        for w in range(count):
            direct.append(remote(shards[w], full[w].at[me], send_sem.at[d, w],
                                 recv_sem.at[d, w], target))
    locals_ = []
    for w in range(count):
        copy = pltpu.make_async_copy(shards[w], full[w].at[me], local_sem.at[w])
        copy.start()
        locals_.append(copy)
        sends.append(remote(shards[w], full[w].at[me], send_sem.at[0, w],
                            recv_sem.at[0, w], sibling))
    for d in range(1, half):
        source = lax.rem(me + n - 2 * d, n)
        for w in range(count):
            direct[(d - 1) * count + w].wait_recv()
            sends.append(remote(full[w].at[source], full[w].at[source], pass_sem.at[0, d, w],
                                pass_sem.at[1, d, w], sibling))
    for copy in direct:
        copy.wait_send()
    for copy in locals_:
        copy.wait()
    for copy in sends:
        copy.wait()


def gather(n, shards, outgoing):
    count = len(shards)
    vmem = pl.BlockSpec(memory_space=pltpu.VMEM)
    shapes = [jax.ShapeDtypeStruct((n, *s.shape), s.dtype) for s in shards]
    shapes.append(jax.ShapeDtypeStruct(outgoing.shape, outgoing.dtype))
    dma = pltpu.SemaphoreType.DMA
    return pl.pallas_call(
        partial(gather_kernel, n, count),
        out_shape=tuple(shapes),
        in_specs=[vmem] * (count + 1),
        out_specs=[vmem] * (count + 1),
        scratch_shapes=[dma((n // 2, count)), dma((n // 2, count)), dma((2, n // 2, count)),
                        dma((count,)), dma((2,)), dma((2,))],
        compiler_params=pltpu.CompilerParams(collective_id=0, has_side_effects=True),
        name="fetch",
    )(*shards, outgoing)


def reduce_kernel(n, depth, count, *refs):
    terms = refs[:count]
    ghosts = refs[count]
    sums = refs[count + 1:2 * count + 1]
    back = refs[2 * count + 1]
    rest = refs[2 * count + 2:]
    landed = rest[:count]
    partial_sums = rest[count:2 * count]
    arrived = rest[2 * count:3 * count]
    layers = rest[3 * count:4 * count]
    core_send, core_recv, chip_send, chip_recv, deep_send, deep_recv, side_send, side_recv = (
        rest[4 * count:])
    me = lax.axis_index("graph")
    row = lax.axis_index("dp")
    half = n // 2
    parity = lax.rem(me, 2)
    chip = lax.div(me, 2)
    sibling = me + 1 - 2 * parity
    right, left = lax.rem(me + 1, n), lax.rem(me + n - 1, n)
    greet(n, depth)

    def remote(src, dst, send, recv, target):
        copy = pltpu.make_async_remote_copy(
            src_ref=src, dst_ref=dst, send_sem=send, recv_sem=recv,
            device_id=target, device_id_type=MESH)
        copy.start()
        return copy

    order = list(range(1, half)) + [0]
    first = {}
    for d in order:
        spot = lax.rem(chip + d, half)
        for w in range(count):
            first[d, w] = remote(
                terms[w].at[2 * spot + 1 - parity], landed[w].at[d],
                core_send.at[d, w], core_recv.at[d, w], (row, sibling))
    sides = [
        remote(ghosts.at[0], back.at[0], side_send.at[0], side_recv.at[0], (row, left)),
        remote(ghosts.at[1], back.at[1], side_send.at[1], side_recv.at[1], (row, right)),
    ]
    second = {}
    for d in order:
        target = lax.rem(me + 2 * d, n)
        for w in range(count):
            first[d, w].wait_recv()
            partial_sums[w][d] = (
                terms[w][target].astype(F32) + landed[w][d].astype(F32)
            ).astype(BF16)
            if d:
                second[d, w] = remote(
                    partial_sums[w].at[d], arrived[w].at[d],
                    chip_send.at[d, w], chip_recv.at[d, w], (row, target))
    third = {}
    for w in range(count):
        total = partial_sums[w][0].astype(F32)
        for d in range(1, half):
            second[d, w].wait_recv()
            total = total + arrived[w][d].astype(F32)
        layers[w][row] = total.astype(BF16)
        for z in range(1, depth):
            third[z, w] = remote(
                layers[w].at[row], layers[w].at[row],
                deep_send.at[z, w], deep_recv.at[z, w], (lax.rem(row + z, depth), me))
    for w in range(count):
        for z in range(1, depth):
            third[z, w].wait_recv()
        total = layers[w][0].astype(F32)
        for z in range(1, depth):
            total = total + layers[w][z].astype(F32)
        sums[w][...] = total
    for group in (first, second, third):
        for copy in group.values():
            copy.wait_send()
    for copy in sides:
        copy.wait()


def reduce(n, depth, terms, ghosts):
    count = len(terms)
    half = n // 2
    vmem = pl.BlockSpec(memory_space=pltpu.VMEM)
    shapes = [jax.ShapeDtypeStruct(t.shape[1:], F32) for t in terms]
    shapes.append(jax.ShapeDtypeStruct(ghosts.shape, ghosts.dtype))
    dma = pltpu.SemaphoreType.DMA
    groups = [half, half, half, depth]
    scratch = [pltpu.VMEM((g, *t.shape[1:]), BF16) for g in groups for t in terms]
    scratch += [dma((half, count)) for _ in range(4)]
    scratch += [dma((depth, count)) for _ in range(2)]
    scratch += [dma((2,)), dma((2,))]
    return pl.pallas_call(
        partial(reduce_kernel, n, depth, count),
        out_shape=tuple(shapes),
        in_specs=[vmem] * (count + 1),
        out_specs=[vmem] * (count + 1),
        scratch_shapes=scratch,
        compiler_params=pltpu.CompilerParams(collective_id=1, has_side_effects=True),
        name="combine",
    )(*terms, ghosts)


def body(n, depth, features, cotangent, rotation, send_left, send_right, edge_src, edge_tgt,
         *weights):
    own = features[0]
    atoms, width = own.shape
    slots = send_left.shape[1]
    head_width, heads = weights[6].shape[0] * n, weights[6].shape[1]
    own_b = own.astype(BF16)
    lists = jnp.concatenate([send_left[0], send_right[0]])
    ids = jnp.arange(atoms, dtype=jnp.int32)
    pick = (lists[:, None] == ids[None, :]).astype(BF16)
    outgoing = jnp.dot(pick, own_b, preferred_element_type=F32).astype(BF16)
    *full, ghosts = gather(n, weights, outgoing.reshape(2, slots, width))
    full = [f.reshape(-1, f.shape[2]) for f in full]
    extended = jnp.concatenate([own_b, ghosts.reshape(2 * slots, width)], axis=0)
    alpha_col = full[6].astype(F32).T.reshape(-1, 1)
    attended, own_grad, ghost_grad, *terms = compute(
        extended, cotangent[0], rotation[0], edge_src, edge_tgt, *full[:6], alpha_col, heads)
    terms[6] = terms[6].reshape(heads, head_width).T.astype(BF16)
    terms = [t.reshape(n, -1, t.shape[1]) for t in terms]
    *grads, back = reduce(n, depth, terms, ghost_grad.reshape(2, slots, width))
    places = jnp.concatenate([send_right[0], send_left[0]])
    put = (ids[:, None] == places[None, :]).astype(BF16)
    grad_features = own_grad + jnp.dot(
        put, back.reshape(2 * slots, width), preferred_element_type=F32)
    return (attended[None], grad_features[None], *grads)


def solution(mesh):
    cell = P("dp", "graph", None)
    lists = P("dp", "graph")
    shard = P("graph", None)
    in_specs = (cell, cell, P("dp", None, "graph")) + (lists,) * 4 + (shard,) * 7
    out_specs = (cell, cell) + (shard,) * 7
    return jax.shard_map(
        partial(body, mesh.shape["graph"], mesh.shape["dp"]), mesh=mesh,
        in_specs=in_specs, out_specs=out_specs, check_vma=False)
```

time: 482 us -> 99.7 us (0.21); the launches traced: 475 us -> 99.2 us
  waiting for transfers between devices: 141 us -> 0 us
  other arithmetic: 119 us -> 5.15 us
  blocking collectives: 95.7 us -> 0 us
  Pallas kernels: 0 us -> 81.1 us
  local copies, waits for them, and re-layouts: 58.4 us -> 9.58 us
  matrix products: 31.6 us -> 2.63 us
  between operations: 22.3 us -> 0.73 us
  starting transfers between devices: 6.1 us -> 0 us
    psum x1 -> x0, waiting for transfers between devices: 141 us -> none  [body(): grand_totals = lax.psum(grad_terms, ('dp', 'graph'))]
    pallas_call x0 -> x3, Pallas kernels: none -> 81.1 us  [the longest x1 45.8 us: reduce(): pl.pallas_call(partial(reduce_kernel, n, depth, count), out_shape=tuple(s...]
    all_gather x6 -> x0, blocking collectives: 55.5 us -> none  [the longest x1 10.2 us: body(): lax.all_gather(w_one_re, 'graph', axis=0, tiled=True)]
    scatter-add x9 -> x0, other arithmetic: 42.8 us -> none  [the longest x4 35.1 us: attend(): jnp.take(coeffs[:, degree * degree:(degree + 1) * (degree + 1), :], edge_...]
    psum x1 -> x0, blocking collectives: 40.2 us -> none  [body(): grand_totals = lax.psum(grad_terms, ('dp', 'graph'))]
    dot_general x36 -> x2, matrix products: 31.6 us -> 2.63 us  [the longest x1 1.77 us: body(): jnp.dot(put, back.reshape(2 * slots, width), preferred_element_type=F32)]
    mul x29 -> x0, other arithmetic: 21.9 us -> none  [the longest x13 17.5 us: apply_block(): total = total + block[row, column][:, None] * source_part[:, column, :]]
    unnamed x26 -> x0, other arithmetic: 15.7 us -> none
  transfers between devices with their start and end apart: 6 -> 0, of which waited for: 1 -> 0; matrix products, arithmetic and copies ran while one was open for 13% -> 0% of each run, Pallas kernels for 0% -> 0%
where the time goes in v1:
time: 99.7 us; the launch traced here: 99.2 us
  Pallas kernels  81.1 us (81%)
  local copies, waits for them, and re-layouts  9.58 us (10%)
  other arithmetic  5.15 us (5%)
  matrix products  2.63 us (3%)
    pallas_call x1, Pallas kernels, reduce(): pl.pallas_call(partial(reduce_kernel, n, depth, count), out_shape=tuple(s...  45.8 us
    pallas_call x1, Pallas kernels, gather(): pl.pallas_call(partial(gather_kernel, n, count), out_shape=tuple(shapes),...  22.8 us
    pallas_call x1, Pallas kernels, compute(): pl.pallas_call(compute_kernel, out_shape=out_shape, in_specs=[vmem] * 12,...  12.5 us
    unnamed x20, local copies, waits for them, and re-layouts  7.8 us

profile of v1, /device:TPU:0, one launch (start us, length us, event | category | flops | bytes accessed | tf_op | source)
XLA Modules:
  0.0 99.2 jit_solution(12822665677621663207)
XLA Ops:
  0.6 0.8 pad_add_fusion.1
  1.5 1.5 %copy.26 = bf16[1,114,192]{2,1,0:T(8,128)(2,1)} copy(bf16[1,114,192]{1,2,0:T(8,128)(2,1)} %param.16) | data formatting | bytes 87552 | tf_op args[2]
  3.0 0.9 convert_bitcast_fusion
  3.9 0.9 fusion.1.refs_7_
  4.8 22.8 %fetch.1 = (bf16[8,80,832]{2,1,0:T(8,128)(2,1)}, bf16[8,64,256]{2,1,0:T(8,128)(2,1)}, bf16[8,64,256]{2,1,0:T(8,128)(2,1)}, bf16[8,48,192]{2,1,0:T(8,128)(2,1)}, ...) custom-call(bf16[80,832]{1,0:T(8,128)(2,1)} %refs_0_.1, ...), custom_call_target="tpu_custom_call" | custom-call | tf_op jit(solution)/shard_map/fetch/pallas_call | solution.py:349
  27.6 1.6 %pad_maximum_fusion.ext_ref = bf16[32,3200]{1,0:T(8,128)(2,1)} fusion(bf16[16,3200]{1,0:T(8,128)(2,1)} %bitcast.49, bf16[16,3200]{1,0:T(8,128)(2,1)S(1)} %convert_bitcast_fusion), kind=kLoop, calls=%fused_computation.4 | loop fusion | flops 409600 | bytes 409600 | tf_op jit(solution)/shard_map/concatenate | solution.py:474
  29.2 0.7 bitcast_convert_fusion
  30.0 0.1 copy.27
  30.0 0.9 reshape.106.alpha_ref
  30.9 12.5 %slab.1 = (bf16[16,1600]{1,0:T(8,128)(2,1)}, f32[16,3200]{1,0:T(8,128)}, bf16[16,3200]{1,0:T(8,128)(2,1)}, bf16[640,832]{1,0:T(8,128)(2,1)}, bf16[512,256]{1,0:T...) custom-call(bf16[32,3200]{1,0:T(8,128)(2,1)} %pad_maximum_fusion.ext, ...), custom_call_target="tpu_custom_call" | custom-call | tf_op jit(solution)/shard_map/slab/pallas_call | solution.py:265
  43.4 1.1 %convert_reduce_fusion = bf16[512]{0:T(512)(128)(2,1)S(1)} fusion(f32[512,1]{1,0:T(8,128)} %get-tuple-element.51), kind=kLoop, calls=%fused_computation.5 | loop fusion | flops 512 | bytes 3072 | tf_op jit(solution)/shard_map/convert_element_type | solution.py:478
  44.5 0.1 convert_element_type.29
  44.6 0.7 copy.29
  45.3 0.0 copy-start
  45.3 45.8 %combine.1 = (f32[80,832]{1,0:T(8,128)}, f32[64,256]{1,0:T(8,128)}, f32[64,256]{1,0:T(8,128)}, f32[48,192]{1,0:T(8,128)}, f32[48,192]{1,0:T(8,128)}, /*index=5*/...) custom-call(bf16[8,80,832]{2,1,0:T(8,128)(2,1)} %bitcast.36, bf16[8,64,256]{2,1,0:T(8,128)(2,1)} %bitcast.37, ...), custom_call_target="tpu_custom_call" | custom-call | tf_op jit(solution)/shard_map/combine/pallas_call | solution.py:450
  91.1 0.0 copy-start.1
  91.2 0.0 copy-start.3
  91.2 0.0 copy-start.2
  91.2 0.0 copy-start.4
  91.2 0.0 copy-start.5
  91.2 0.0 copy-done
  91.2 1.8 %fusion = f32[1,16,3200]{2,1,0:T(8,128)} fusion(f32[16,3200]{1,0:T(8,128)S(1)} %copy-done, bf16[2,8,3200]{2,1,0:T(8,128)(2,1)} %get-tuple-element.53, s32[16]{0:T(128)S(1)} %get-tuple-element.61), kind=kOutput, calls=%fused_computation.1 | convolution fusion | flops 1689856 | bytes 512064 | tf_op jit(solution)/shard_map/dot_general | solution.py:483
  93.0 1.7 %copy.37 = f32[80,832]{1,0:T(8,128)} copy(f32[80,832]{1,0:T(8,128)} %get-tuple-element.74) | data formatting | bytes 532480
  94.7 1.5 %copy.38 = f32[64,256]{1,0:T(8,128)} copy(f32[64,256]{1,0:T(8,128)} %get-tuple-element.75) | data formatting | bytes 131072
  96.1 0.0 copy-done.1
  96.1 0.6 copy.39
  96.8 0.0 copy-done.3
  96.8 0.6 copy.40
  97.4 0.0 copy-done.2
  97.4 0.6 copy.41
  98.0 0.0 copy-done.4
  98.0 0.6 copy.42
  98.6 0.0 copy-done.5
  98.6 0.6 copy.43
Async XLA Ops:
  45.3 45.9 %copy-start = (f32[16,3200]{1,0:T(8,128)S(1)}, f32[16,3200]{1,0:T(8,128)}, u32[]{:S(2)}) copy-start(f32[16,3200]{1,0:T(8,128)} %get-tuple-element.44) | copy-start | bytes 614404
  91.1 5.0 %copy-start.1 = (f32[64,256]{1,0:T(8,128)S(1)}, f32[64,256]{1,0:T(8,128)}, u32[]{:S(2)}) copy-start(f32[64,256]{1,0:T(8,128)} %get-tuple-element.76) | copy-start | bytes 196612
  91.2 5.6 %copy-start.3 = (f32[48,192]{1,0:T(8,128)S(1)}, f32[48,192]{1,0:T(8,128)}, u32[]{:S(2)}) copy-start(f32[48,192]{1,0:T(8,128)} %get-tuple-element.77) | copy-start | bytes 110596
  91.2 6.2 %copy-start.2 = (f32[48,192]{1,0:T(8,128)S(1)}, f32[48,192]{1,0:T(8,128)}, u32[]{:S(2)}) copy-start(f32[48,192]{1,0:T(8,128)} %get-tuple-element.78) | copy-start | bytes 110596
  91.2 6.8 %copy-start.4 = (f32[16,512]{1,0:T(8,128)S(1)}, f32[16,512]{1,0:T(8,128)}, u32[]{:S(2)}) copy-start(f32[16,512]{1,0:T(8,128)} %get-tuple-element.79) | copy-start | bytes 98308
  91.2 7.4 %copy-start.5 = (f32[8,8]{1,0:T(8,128)S(1)}, f32[8,8]{1,0:T(8,128)}, u32[]{:S(2)}) copy-start(f32[8,8]{1,0:T(8,128)} %get-tuple-element.80) | copy-start | bytes 772

commit v2 on v1

--- a/solution.py
+++ b/solution.py
@@ -35,10 +35,10 @@
 
 
 def compute_kernel(
-    ext_ref, cot_ref, rotation_ref, src_ref, tgt_ref,
+    feat_ref, near_ref, cot_ref, rotation_ref, src_ref, tgt_ref,
     wz_ref, w1r_ref, w1i_ref, w2r_ref, w2i_ref, wt_ref, alpha_ref,
     att_ref, own_ref, ghost_ref, gz_ref, g1r_ref, g1i_ref, g2r_ref, g2i_ref, gt_ref, ga_ref,
-    rotf, xs, turned, hid, msg, dmsg, scores, dhid, dmixed, dturned, dxs, small, spreads,
+    ext_ref, alphas, d_alphas, rotf, xs, turned, hid, msg, dmsg, scores, dhid, dmixed, dturned, dxs, small, spreads,
 ):
     edges = rotation_ref.shape[1]
     rows = ext_ref.shape[0]
@@ -46,7 +46,13 @@
     channels = wt_ref.shape[0]
     hidden = w1r_ref.shape[1] // 4
     heads = small.shape[1]
-    width = alpha_ref.shape[0] // heads
+    width = alphas.shape[0]
+    pieces, piece_rows = alpha_ref.shape[:2]
+
+    ext_ref[:atoms, :] = feat_ref[...].astype(BF16)
+    ext_ref[atoms:, :] = near_ref[...].astype(F32).reshape(rows - atoms, -1).astype(BF16)
+    for j in range(pieces):
+        alphas[j * piece_rows:(j + 1) * piece_rows, :] = alpha_ref[j].astype(F32)
 
     rotf[...] = rotation_ref[...].astype(F32)
     src_hot = (
@@ -109,7 +115,7 @@
         scores[part, :] = normed
         gate = 0.2 + 0.8 * jax.nn.sigmoid(normed)
         small[0, h:h + 1, :] = jnp.sum(
-            normed * gate * alpha_ref[part, :], axis=0, keepdims=True
+            normed * gate * alphas[:, h:h + 1], axis=0, keepdims=True
         )
         small[1, h:h + 1, :] = scale
 
@@ -174,15 +180,18 @@
         sig = jax.nn.sigmoid(normed)
         gate = 0.2 + 0.8 * sig
         d_logit = small[0, h:h + 1, :]
-        ga_ref[part, :] = jnp.sum(normed * gate * d_logit, axis=1, keepdims=True)
-        d_norm = d_logit * alpha_ref[part, :] * (gate + 0.8 * normed * sig * (1.0 - sig))
+        d_alphas[:, h:h + 1] = jnp.sum(normed * gate * d_logit, axis=1, keepdims=True)
+        d_norm = d_logit * alphas[:, h:h + 1] * (gate + 0.8 * normed * sig * (1.0 - sig))
         first = jnp.mean(d_norm, axis=0, keepdims=True)
         second = jnp.mean(d_norm * normed, axis=0, keepdims=True)
         d_score = small[1, h:h + 1, :] * (d_norm - first - normed * second)
         dmixed[5 * hidden + h * width:5 * hidden + (h + 1) * width, :] = d_score.astype(BF16)
+        scores[part, :] = d_score
+    for j in range(pieces):
+        ga_ref[j] = d_alphas[j * piece_rows:(j + 1) * piece_rows, :].astype(BF16)
     dmixed[:5 * hidden, :] = dhid[0:5].reshape(5 * hidden, edges)
 
-    d_per_atom = dot(member_b, dmixed[5 * hidden:, :], 1, 1).astype(BF16)
+    d_per_atom = dot(member, scores[...], 1, 1, exact).astype(BF16)
     gt_ref[...] = dot(ext_ref[:atoms, :channels], d_per_atom, 0, 0).astype(BF16)
     d_target = dot(d_per_atom, wt_ref[...], 1, 1)
 
@@ -224,13 +233,17 @@
     ext_grad = dot(src_hot, dxs[...].reshape(25 * channels, edges), 1, 1)
     own_ref[...] = ext_grad[:atoms]
     own_ref[:, :channels] = ext_grad[:atoms, :channels] + d_target
-    ghost_ref[...] = ext_grad[atoms:].astype(BF16)
-
-
-def compute(ext, cot, rotation, src, tgt, wz, w1r, w1i, w2r, w2i, wt, alpha_col, heads):
+    slots = ghost_ref.shape[1]
+    for side in range(2):
+        begin = atoms + side * slots
+        ghost_ref[side] = ext_grad[begin:begin + slots].astype(BF16)
+
+
+def compute(features, near, cot, rotation, src, tgt, wz, w1r, w1i, w2r, w2i, wt, alpha):
     edges = rotation.shape[1]
     atoms = cot.shape[0]
-    ghosts = ext.shape[0] - atoms
+    pieces, piece_rows, heads = alpha.shape
+    head_width = pieces * piece_rows
     channels = wt.shape[0]
     hidden = w1r.shape[1] // 4
     shape = jax.ShapeDtypeStruct
@@ -238,23 +251,26 @@
     out_shape = (
         shape((atoms, 25 * hidden), BF16),
         shape((atoms, 25 * channels), F32),
-        shape((ghosts, 25 * channels), BF16),
+        shape(near.shape, BF16),
         shape(wz.shape, BF16),
         shape(w1r.shape, BF16),
         shape(w1i.shape, BF16),
         shape(w2r.shape, BF16),
         shape(w2i.shape, BF16),
         shape(wt.shape, BF16),
-        shape(alpha_col.shape, F32),
+        shape(alpha.shape, BF16),
     )
     scratch = [
+        pltpu.VMEM((atoms + 2 * near.shape[1], 25 * channels), BF16),
+        pltpu.VMEM((head_width, heads), F32),
+        pltpu.VMEM((head_width, heads), F32),
         pltpu.VMEM(rotation.shape, F32),
         pltpu.VMEM((25, channels, edges), F32),
         pltpu.VMEM((19, channels, edges), BF16),
         pltpu.VMEM((19, hidden, edges), F32),
         pltpu.VMEM((25, hidden, edges), BF16),
         pltpu.VMEM((25, hidden, edges), F32),
-        pltpu.VMEM((alpha_col.shape[0], edges), F32),
+        pltpu.VMEM((head_width * heads, edges), F32),
         pltpu.VMEM((19, hidden, edges), BF16),
         pltpu.VMEM((wz.shape[1], edges), BF16),
         pltpu.VMEM((19, channels, edges), F32),
@@ -265,12 +281,12 @@
     return pl.pallas_call(
         compute_kernel,
         out_shape=out_shape,
-        in_specs=[vmem] * 12,
+        in_specs=[vmem] * 13,
         out_specs=[vmem] * 10,
         scratch_shapes=scratch,
         compiler_params=pltpu.CompilerParams(vmem_limit_bytes=56 * 2**20),
         name="slab",
-    )(ext, cot, rotation, src, tgt, wz, w1r, w1i, w2r, w2i, wt, alpha_col)
+    )(features, near, cot, rotation, src, tgt, wz, w1r, w1i, w2r, w2i, wt, alpha)
 
 
 MESH = pl.DeviceIdType.MESH
@@ -291,15 +307,20 @@
 
 def gather_kernel(n, count, *refs):
     shards = refs[:count]
-    outgoing = refs[count]
-    full = refs[count + 1:2 * count + 1]
-    ghosts = refs[2 * count + 1]
-    send_sem, recv_sem, pass_sem, local_sem, side_send, side_recv = refs[2 * count + 2:]
+    feat_ref, left_ref, right_ref = refs[count:count + 3]
+    full = refs[count + 3:2 * count + 3]
+    ghosts = refs[2 * count + 3]
+    outgoing, send_sem, recv_sem, pass_sem, local_sem, side_send, side_recv = refs[2 * count + 4:]
     me = lax.axis_index("graph")
     row = lax.axis_index("dp")
     half = n // 2
     sibling = me + 1 - 2 * lax.rem(me, 2)
     right, left = lax.rem(me + 1, n), lax.rem(me + n - 1, n)
+    own = feat_ref[...].astype(BF16)
+    for side, list_ref in ((0, left_ref), (1, right_ref)):
+        ids = lax.broadcasted_iota(jnp.int32, (own.shape[0], list_ref.shape[1]), 0)
+        pick = (ids == list_ref[...]).astype(F32).astype(BF16)
+        outgoing[side] = dot(pick, own, 0, 0).astype(BF16)
     greet(n, 1)
 
     def remote(src, dst, send, recv, target):
@@ -310,9 +331,6 @@
         return copy
 
     sends = []
-    for side, target in ((1, left), (0, right)):
-        sends.append(remote(outgoing.at[1 - side], ghosts.at[side], side_send.at[side],
-                            side_recv.at[side], target))
     direct = []
     for d in range(1, half):
         target = lax.rem(me + 2 * d, n)
@@ -326,6 +344,9 @@
         locals_.append(copy)
         sends.append(remote(shards[w], full[w].at[me], send_sem.at[0, w],
                             recv_sem.at[0, w], sibling))
+    for side, target in ((1, left), (0, right)):
+        sends.append(remote(outgoing.at[1 - side], ghosts.at[side], side_send.at[side],
+                            side_recv.at[side], target))
     for d in range(1, half):
         source = lax.rem(me + n - 2 * d, n)
         for w in range(count):
@@ -340,36 +361,39 @@
         copy.wait()
 
 
-def gather(n, shards, outgoing):
+def gather(n, shards, features, send_left, send_right):
     count = len(shards)
     vmem = pl.BlockSpec(memory_space=pltpu.VMEM)
     shapes = [jax.ShapeDtypeStruct((n, *s.shape), s.dtype) for s in shards]
-    shapes.append(jax.ShapeDtypeStruct(outgoing.shape, outgoing.dtype))
+    ghosts = (2, send_left.shape[1], features.shape[1])
+    shapes.append(jax.ShapeDtypeStruct(ghosts, BF16))
     dma = pltpu.SemaphoreType.DMA
     return pl.pallas_call(
         partial(gather_kernel, n, count),
         out_shape=tuple(shapes),
-        in_specs=[vmem] * (count + 1),
+        in_specs=[vmem] * (count + 3),
         out_specs=[vmem] * (count + 1),
-        scratch_shapes=[dma((n // 2, count)), dma((n // 2, count)), dma((2, n // 2, count)),
+        scratch_shapes=[pltpu.VMEM(ghosts, BF16),
+                        dma((n // 2, count)), dma((n // 2, count)), dma((2, n // 2, count)),
                         dma((count,)), dma((2,)), dma((2,))],
         compiler_params=pltpu.CompilerParams(collective_id=0, has_side_effects=True),
         name="fetch",
-    )(*shards, outgoing)
+    )(*shards, features, send_left, send_right)
 
 
 def reduce_kernel(n, depth, count, *refs):
     terms = refs[:count]
     ghosts = refs[count]
-    sums = refs[count + 1:2 * count + 1]
+    final = refs[count + 1:2 * count + 1]
     back = refs[2 * count + 1]
     rest = refs[2 * count + 2:]
     landed = rest[:count]
     partial_sums = rest[count:2 * count]
     arrived = rest[2 * count:3 * count]
     layers = rest[3 * count:4 * count]
-    core_send, core_recv, chip_send, chip_recv, deep_send, deep_recv, side_send, side_recv = (
-        rest[4 * count:])
+    incoming = rest[4 * count:5 * count]
+    (core_send, core_recv, chip_send, chip_recv, deep_send, deep_recv, last_send, last_recv,
+     side_send, side_recv) = rest[5 * count:]
     me = lax.axis_index("graph")
     row = lax.axis_index("dp")
     half = n // 2
@@ -387,21 +411,16 @@
         return copy
 
     order = list(range(1, half)) + [0]
-    first = {}
-    for d in order:
-        spot = lax.rem(chip + d, half)
-        for w in range(count):
+    first, second, third, fourth = {}, {}, {}, {}
+    for w in range(count):
+        for d in order:
+            spot = lax.rem(chip + d, half)
             first[d, w] = remote(
                 terms[w].at[2 * spot + 1 - parity], landed[w].at[d],
                 core_send.at[d, w], core_recv.at[d, w], (row, sibling))
-    sides = [
-        remote(ghosts.at[0], back.at[0], side_send.at[0], side_recv.at[0], (row, left)),
-        remote(ghosts.at[1], back.at[1], side_send.at[1], side_recv.at[1], (row, right)),
-    ]
-    second = {}
-    for d in order:
-        target = lax.rem(me + 2 * d, n)
-        for w in range(count):
+    for w in range(count):
+        for d in order:
+            target = lax.rem(me + 2 * d, n)
             first[d, w].wait_recv()
             partial_sums[w][d] = (
                 terms[w][target].astype(F32) + landed[w][d].astype(F32)
@@ -410,42 +429,64 @@
                 second[d, w] = remote(
                     partial_sums[w].at[d], arrived[w].at[d],
                     chip_send.at[d, w], chip_recv.at[d, w], (row, target))
-    third = {}
+    sides = [
+        remote(ghosts.at[0], back.at[0], side_send.at[0], side_recv.at[0], (row, left)),
+        remote(ghosts.at[1], back.at[1], side_send.at[1], side_recv.at[1], (row, right)),
+    ]
+    split = [final[w].shape[1] != terms[w].shape[1]
+             for w in range(count)]
     for w in range(count):
         total = partial_sums[w][0].astype(F32)
         for d in range(1, half):
             second[d, w].wait_recv()
             total = total + arrived[w][d].astype(F32)
-        layers[w][row] = total.astype(BF16)
+        if split[w]:
+            size = total.shape[0] // depth
+            for k in range(depth):
+                layers[w][k] = total[k * size:(k + 1) * size].astype(BF16)
+            for z in range(1, depth):
+                target = lax.rem(row + z, depth)
+                third[z, w] = remote(
+                    layers[w].at[target], incoming[w].at[z],
+                    deep_send.at[z, w], deep_recv.at[z, w], (target, me))
+        else:
+            final[w][row] = total.astype(BF16)
+    for w in range(count):
+        if split[w]:
+            total = layers[w][row].astype(F32)
+            for z in range(1, depth):
+                third[z, w].wait_recv()
+                total = total + incoming[w][z].astype(F32)
+            final[w][row] = total.astype(BF16)
         for z in range(1, depth):
-            third[z, w] = remote(
-                layers[w].at[row], layers[w].at[row],
-                deep_send.at[z, w], deep_recv.at[z, w], (lax.rem(row + z, depth), me))
-    for w in range(count):
-        for z in range(1, depth):
-            third[z, w].wait_recv()
-        total = layers[w][0].astype(F32)
-        for z in range(1, depth):
-            total = total + layers[w][z].astype(F32)
-        sums[w][...] = total
+            fourth[z, w] = remote(
+                final[w].at[row], final[w].at[row],
+                last_send.at[z, w], last_recv.at[z, w], (lax.rem(row + z, depth), me))
     for group in (first, second, third):
         for copy in group.values():
             copy.wait_send()
     for copy in sides:
         copy.wait()
+    for copy in fourth.values():
+        copy.wait()
 
 
 def reduce(n, depth, terms, ghosts):
     count = len(terms)
     half = n // 2
     vmem = pl.BlockSpec(memory_space=pltpu.VMEM)
-    shapes = [jax.ShapeDtypeStruct(t.shape[1:], F32) for t in terms]
+
+    def layered(t):
+        rows = t.shape[1] if t.shape[1] % depth else t.shape[1] // depth
+        return (depth, rows, t.shape[2])
+
+    shapes = [jax.ShapeDtypeStruct(layered(t), BF16) for t in terms]
     shapes.append(jax.ShapeDtypeStruct(ghosts.shape, ghosts.dtype))
     dma = pltpu.SemaphoreType.DMA
-    groups = [half, half, half, depth]
-    scratch = [pltpu.VMEM((g, *t.shape[1:]), BF16) for g in groups for t in terms]
+    scratch = [pltpu.VMEM((half, *t.shape[1:]), BF16) for _ in range(3) for t in terms]
+    scratch += [pltpu.VMEM(layered(t), BF16) for _ in range(2) for t in terms]
     scratch += [dma((half, count)) for _ in range(4)]
-    scratch += [dma((depth, count)) for _ in range(2)]
+    scratch += [dma((depth, count)) for _ in range(4)]
     scratch += [dma((2,)), dma((2,))]
     return pl.pallas_call(
         partial(reduce_kernel, n, depth, count),
@@ -458,30 +499,52 @@
     )(*terms, ghosts)
 
 
+def finish_kernel(count, *refs):
+    own_ref, back_ref, left_ref, right_ref = refs[:4]
+    final = refs[4:4 + count]
+    out_ref = refs[4 + count]
+    grads = refs[5 + count:]
+    total = own_ref[...]
+    for side, list_ref in ((0, right_ref), (1, left_ref)):
+        ids = lax.broadcasted_iota(jnp.int32, (total.shape[0], list_ref.shape[1]), 0)
+        put = (ids == list_ref[...]).astype(F32).astype(BF16)
+        total = total + dot(put, back_ref[side], 1, 0)
+    out_ref[...] = total
+    for source, grad in zip(final, grads):
+        depth, size = source.shape[:2]
+        if size == grad.shape[0]:
+            value = source[0].astype(F32)
+            for k in range(1, depth):
+                value = value + source[k].astype(F32)
+            grad[...] = value
+        else:
+            for k in range(depth):
+                grad[k * size:(k + 1) * size, :] = source[k].astype(F32)
+
+
+def finish(own, back, send_left, send_right, final, weights):
+    count = len(final)
+    vmem = pl.BlockSpec(memory_space=pltpu.VMEM)
+    shapes = [jax.ShapeDtypeStruct(own.shape, F32)]
+    shapes += [jax.ShapeDtypeStruct(w.shape, F32) for w in weights]
+    return pl.pallas_call(
+        partial(finish_kernel, count),
+        out_shape=tuple(shapes),
+        in_specs=[vmem] * (count + 4),
+        out_specs=[vmem] * (count + 1),
+        name="finish",
+    )(own, back, send_left, send_right, *final)
+
+
 def body(n, depth, features, cotangent, rotation, send_left, send_right, edge_src, edge_tgt,
          *weights):
-    own = features[0]
-    atoms, width = own.shape
-    slots = send_left.shape[1]
-    head_width, heads = weights[6].shape[0] * n, weights[6].shape[1]
-    own_b = own.astype(BF16)
-    lists = jnp.concatenate([send_left[0], send_right[0]])
-    ids = jnp.arange(atoms, dtype=jnp.int32)
-    pick = (lists[:, None] == ids[None, :]).astype(BF16)
-    outgoing = jnp.dot(pick, own_b, preferred_element_type=F32).astype(BF16)
-    *full, ghosts = gather(n, weights, outgoing.reshape(2, slots, width))
-    full = [f.reshape(-1, f.shape[2]) for f in full]
-    extended = jnp.concatenate([own_b, ghosts.reshape(2 * slots, width)], axis=0)
-    alpha_col = full[6].astype(F32).T.reshape(-1, 1)
+    *full, near = gather(n, weights, features[0], send_left, send_right)
+    matrices = [f.reshape(-1, f.shape[2]) for f in full[:6]]
     attended, own_grad, ghost_grad, *terms = compute(
-        extended, cotangent[0], rotation[0], edge_src, edge_tgt, *full[:6], alpha_col, heads)
-    terms[6] = terms[6].reshape(heads, head_width).T.astype(BF16)
-    terms = [t.reshape(n, -1, t.shape[1]) for t in terms]
-    *grads, back = reduce(n, depth, terms, ghost_grad.reshape(2, slots, width))
-    places = jnp.concatenate([send_right[0], send_left[0]])
-    put = (ids[:, None] == places[None, :]).astype(BF16)
-    grad_features = own_grad + jnp.dot(
-        put, back.reshape(2 * slots, width), preferred_element_type=F32)
+        features[0], near, cotangent[0], rotation[0], edge_src, edge_tgt, *matrices, full[6])
+    terms = [t.reshape(n, -1, t.shape[-1]) for t in terms]
+    *final, back = reduce(n, depth, terms, ghost_grad)
+    grad_features, *grads = finish(own_grad, back, send_left, send_right, final, weights)
     return (attended[None], grad_features[None], *grads)
 
 

time: 99.7 us -> 73.4 us (0.74)
  Pallas kernels: 81.1 us -> 70.9 us
  local copies, waits for them, and re-layouts: 9.58 us -> 1.54 us
  other arithmetic: 5.15 us -> 0 us
  matrix products: 2.63 us -> 0 us
    pallas_call x1, Pallas kernels: 45.8 us -> 33.3 us  [reduce(): pl.pallas_call(partial(reduce_kernel, n, depth, count), out_shape=tuple(s...]
    unnamed x20 -> x1, local copies, waits for them, and re-layouts: 7.8 us -> 1.54 us
    dot_general x2 -> x0, matrix products: 2.63 us -> none  [the longest x1 1.77 us: body(): jnp.dot(put, back.reshape(2 * slots, width), preferred_element_type=F32)]
    concatenate x2 -> x0, other arithmetic: 2.4 us -> none  [the longest x1 1.59 us: body(): jnp.concatenate([own_b, ghosts.reshape(2 * slots, width)], axis=0)]
    pallas_call x1 -> x2, Pallas kernels: 12.5 us -> 14.7 us  [the longest x1 12.6 us: compute(): pl.pallas_call(compute_kernel, out_shape=out_shape, in_specs=[vmem] * 13,...]
    convert_element_type x2 -> x0, other arithmetic: 2.03 us -> none  [the longest x1 1.09 us: body(): terms[6] = terms[6].reshape(heads, head_width).T.astype(BF16)]
where the time goes in v2:
time: 73.4 us; the launch traced here: 73.1 us
  Pallas kernels  70.9 us (97%)
  local copies, waits for them, and re-layouts  1.54 us (2%)
    pallas_call x1, Pallas kernels, reduce(): pl.pallas_call(partial(reduce_kernel, n, depth, count), out_shape=tuple(s...  33.3 us
    pallas_call x1, Pallas kernels, gather(): pl.pallas_call(partial(gather_kernel, n, count), out_shape=tuple(shapes),...  22.8 us
    pallas_call x1, Pallas kernels, compute(): pl.pallas_call(compute_kernel, out_shape=out_shape, in_specs=[vmem] * 13,...  12.6 us
    pallas_call x1, Pallas kernels, finish(): pl.pallas_call(partial(finish_kernel, count), out_shape=tuple(shapes), in...  2.12 us
    unnamed x1, local copies, waits for them, and re-layouts  1.54 us

profile of v2, /device:TPU:0, one launch (start us, length us, event | category | flops | bytes accessed | tf_op | source)
XLA Modules:
  0.0 73.1 jit_solution(104978608375092961)
XLA Ops:
  0.6 1.5 %copy.23 = bf16[1,114,192]{2,1,0:T(8,128)(2,1)} copy(bf16[1,114,192]{1,2,0:T(8,128)(2,1)} %param.16) | data formatting | bytes 87552 | tf_op args[2]
  2.2 22.8 %fetch.1 = (bf16[8,80,832]{2,1,0:T(8,128)(2,1)}, bf16[8,64,256]{2,1,0:T(8,128)(2,1)}, bf16[8,64,256]{2,1,0:T(8,128)(2,1)}, bf16[8,48,192]{2,1,0:T(8,128)(2,1)}, ...) custom-call(bf16[80,832]{1,0:T(8,128)(2,1)} %refs_0_.1, ...), custom_call_target="tpu_custom_call" | custom-call | tf_op jit(solution)/shard_map/fetch/pallas_call | solution.py:371
  25.0 12.6 %slab.1 = (bf16[16,1600]{1,0:T(8,128)(2,1)}, f32[16,3200]{1,0:T(8,128)}, bf16[2,8,3200]{2,1,0:T(8,128)(2,1)}, bf16[640,832]{1,0:T(8,128)(2,1)}, bf16[512,256]{1,...) custom-call(f32[16,3200]{1,0:T(8,128)} %bitcast.20, ...), custom_call_target="tpu_custom_call" | custom-call | tf_op jit(solution)/shard_map/slab/pallas_call | solution.py:281
  37.6 33.3 %combine.1 = (bf16[4,20,832]{2,1,0:T(8,128)(2,1)}, bf16[4,16,256]{2,1,0:T(8,128)(2,1)}, bf16[4,16,256]{2,1,0:T(8,128)(2,1)}, bf16[4,12,192]{2,1,0:T(8,128)(2,1)}...) custom-call(bf16[8,80,832]{2,1,0:T(8,128)(2,1)} %bitcast.17, ...), custom_call_target="tpu_custom_call" | custom-call | tf_op jit(solution)/shard_map/combine/pallas_call | solution.py:491
  71.0 2.1 %finish.1 = (f32[16,3200]{1,0:T(8,128)}, f32[80,832]{1,0:T(8,128)}, f32[64,256]{1,0:T(8,128)}, f32[64,256]{1,0:T(8,128)}, f32[48,192]{1,0:T(8,128)}, /*index=5*/...) custom-call(f32[16,3200]{1,0:T(8,128)} %get-tuple-element.52.refs_0_, bf16[2,8,3200]{2,1,0:T(8,128)(2,1)} %get-tuple-element.61.refs_1_, ...), custom_call_target="tpu_custom_call" | custom-call | tf_op jit(solution)/shard_map/finish/pallas_call | solution.py:530

commit v3 on v2

--- a/solution.py
+++ b/solution.py
@@ -40,7 +40,7 @@
     att_ref, own_ref, ghost_ref, gz_ref, g1r_ref, g1i_ref, g2r_ref, g2i_ref, gt_ref, ga_ref,
     ext_ref, alphas, d_alphas, rotf, xs, turned, hid, msg, dmsg, scores, dhid, dmixed, dturned, dxs, small, spreads,
 ):
-    edges = rotation_ref.shape[1]
+    edges, entries = rotation_ref.shape
     rows = ext_ref.shape[0]
     atoms = att_ref.shape[0]
     channels = wt_ref.shape[0]
@@ -54,7 +54,11 @@
     for j in range(pieces):
         alphas[j * piece_rows:(j + 1) * piece_rows, :] = alpha_ref[j].astype(F32)
 
-    rotf[...] = rotation_ref[...].astype(F32)
+    diagonal = (
+        lax.broadcasted_iota(jnp.int32, (entries, entries), 0)
+        == lax.broadcasted_iota(jnp.int32, (entries, entries), 1)
+    ).astype(F32).astype(BF16)
+    rotf[...] = dot(diagonal, rotation_ref[...], 1, 1)
     src_hot = (
         lax.broadcasted_iota(jnp.int32, (rows, edges), 0) == src_ref[...]
     ).astype(F32).astype(BF16)
@@ -240,7 +244,7 @@
 
 
 def compute(features, near, cot, rotation, src, tgt, wz, w1r, w1i, w2r, w2i, wt, alpha):
-    edges = rotation.shape[1]
+    edges, entries = rotation.shape
     atoms = cot.shape[0]
     pieces, piece_rows, heads = alpha.shape
     head_width = pieces * piece_rows
@@ -264,7 +268,7 @@
         pltpu.VMEM((atoms + 2 * near.shape[1], 25 * channels), BF16),
         pltpu.VMEM((head_width, heads), F32),
         pltpu.VMEM((head_width, heads), F32),
-        pltpu.VMEM(rotation.shape, F32),
+        pltpu.VMEM((entries, edges), F32),
         pltpu.VMEM((25, channels, edges), F32),
         pltpu.VMEM((19, channels, edges), BF16),
         pltpu.VMEM((19, hidden, edges), F32),
@@ -435,7 +439,7 @@
     ]
     split = [final[w].shape[1] != terms[w].shape[1]
              for w in range(count)]
-    for w in range(count):
+    def sum_chips(w):
         total = partial_sums[w][0].astype(F32)
         for d in range(1, half):
             second[d, w].wait_recv()
@@ -451,7 +455,8 @@
                     deep_send.at[z, w], deep_recv.at[z, w], (target, me))
         else:
             final[w][row] = total.astype(BF16)
-    for w in range(count):
+
+    def sum_depth(w):
         if split[w]:
             total = layers[w][row].astype(F32)
             for z in range(1, depth):
@@ -462,6 +467,13 @@
             fourth[z, w] = remote(
                 final[w].at[row], final[w].at[row],
                 last_send.at[z, w], last_recv.at[z, w], (lax.rem(row + z, depth), me))
+
+    lag = min(4, count)
+    for w in range(count + lag):
+        if w < count:
+            sum_chips(w)
+        if w >= lag:
+            sum_depth(w - lag)
     for group in (first, second, third):
         for copy in group.values():
             copy.wait_send()
@@ -541,7 +553,7 @@
     *full, near = gather(n, weights, features[0], send_left, send_right)
     matrices = [f.reshape(-1, f.shape[2]) for f in full[:6]]
     attended, own_grad, ghost_grad, *terms = compute(
-        features[0], near, cotangent[0], rotation[0], edge_src, edge_tgt, *matrices, full[6])
+        features[0], near, cotangent[0], rotation[0].T, edge_src, edge_tgt, *matrices, full[6])
     terms = [t.reshape(n, -1, t.shape[-1]) for t in terms]
     *final, back = reduce(n, depth, terms, ghost_grad)
     grad_features, *grads = finish(own_grad, back, send_left, send_right, final, weights)

time: 73.4 us -> 75.1 us (1.023)
  Pallas kernels: 70.9 us -> 74.2 us
  local copies, waits for them, and re-layouts: 1.54 us -> 0 us
    pallas_call x1, Pallas kernels: 33.3 us -> 36.7 us  [reduce(): pl.pallas_call(partial(reduce_kernel, n, depth, count), out_shape=tuple(s...]
    unnamed x1 -> x0, local copies, waits for them, and re-layouts: 1.54 us -> none
where the time goes in v3:
time: 75.1 us; the launch traced here: 74.9 us
  Pallas kernels  74.2 us (99%)
    pallas_call x1, Pallas kernels, reduce(): pl.pallas_call(partial(reduce_kernel, n, depth, count), out_shape=tuple(s...  36.7 us
    pallas_call x1, Pallas kernels, gather(): pl.pallas_call(partial(gather_kernel, n, count), out_shape=tuple(shapes),...  22.9 us
    pallas_call x1, Pallas kernels, compute(): pl.pallas_call(compute_kernel, out_shape=out_shape, in_specs=[vmem] * 13,...  12.5 us
    pallas_call x1, Pallas kernels, finish(): pl.pallas_call(partial(finish_kernel, count), out_shape=tuple(shapes), in...  2.12 us

profile of v3, /device:TPU:0, one launch (start us, length us, event | category | flops | bytes accessed | tf_op | source)
XLA Modules:
  0.0 74.9 jit_solution(17107216077025203124)
XLA Ops:
  0.6 22.9 %fetch.1 = (bf16[8,80,832]{2,1,0:T(8,128)(2,1)}, bf16[8,64,256]{2,1,0:T(8,128)(2,1)}, bf16[8,64,256]{2,1,0:T(8,128)(2,1)}, bf16[8,48,192]{2,1,0:T(8,128)(2,1)}, ...) custom-call(bf16[80,832]{1,0:T(8,128)(2,1)} %refs_0_.1, ...), custom_call_target="tpu_custom_call" | custom-call | tf_op jit(solution)/shard_map/fetch/pallas_call | solution.py:375
  23.5 12.5 %slab.1 = (bf16[16,1600]{1,0:T(8,128)(2,1)}, f32[16,3200]{1,0:T(8,128)}, bf16[2,8,3200]{2,1,0:T(8,128)(2,1)}, bf16[640,832]{1,0:T(8,128)(2,1)}, bf16[512,256]{1,...) custom-call(f32[16,3200]{1,0:T(8,128)} %bitcast.22, ...), custom_call_target="tpu_custom_call" | custom-call | tf_op jit(solution)/shard_map/slab/pallas_call | solution.py:285
  36.1 36.7 %combine.1 = (bf16[4,20,832]{2,1,0:T(8,128)(2,1)}, bf16[4,16,256]{2,1,0:T(8,128)(2,1)}, bf16[4,16,256]{2,1,0:T(8,128)(2,1)}, bf16[4,12,192]{2,1,0:T(8,128)(2,1)}...) custom-call(bf16[8,80,832]{2,1,0:T(8,128)(2,1)} %bitcast.20, ...), custom_call_target="tpu_custom_call" | custom-call | tf_op jit(solution)/shard_map/combine/pallas_call | solution.py:503
  72.7 2.1 %finish.1 = (f32[16,3200]{1,0:T(8,128)}, f32[80,832]{1,0:T(8,128)}, f32[64,256]{1,0:T(8,128)}, f32[64,256]{1,0:T(8,128)}, f32[48,192]{1,0:T(8,128)}, /*index=5*/...) custom-call(f32[16,3200]{1,0:T(8,128)} %get-tuple-element.52.refs_0_, bf16[2,8,3200]{2,1,0:T(8,128)(2,1)} %get-tuple-element.61.refs_1_, ...), custom_call_target="tpu_custom_call" | custom-call | tf_op jit(solution)/shard_map/finish/pallas_call | solution.py:542
